TPU v7x, 256 devices: a whole 4x4x8 slice. The times are simulated.
256 devices in a mesh: row: 8 (over y_lo, x), col: 32 (over z, y_hi, core).
Axes of the slice: x: 4, y: 4 (y_hi: 2, y_lo: 2; y = y_hi * 2 + y_lo), z: 8, core: 2. Of those that a mesh axis runs over, the one named last changes fastest.
Arguments:
- points: float32 [32768, 128], P(('row', 'col')), may hold values from -4 to 4
- labels: int32 [32768], P(('row', 'col')), may hold values from 0 to 63
- coefficients: float32 [32768, 64], P(('row', 'col')), as said below
Outputs:
- new_coefficients: float32 [32768, 64], P(('row', 'col'))
- probabilities: float32 [32768, 64], P(('row', 'col'))
Inputs may be any that keep to these rules, and one draw needn't show every extreme that they name: `coefficients`: entries have magnitude at most 300 * sqrt(32768) / 16.
All inputs are finite; a program needn't handle non-finite values.
Results may differ from a plain program's by a relative error of at most 0.012.
The roundings to bfloat16 on the way count: a program that leaves them out, or rounds other values in their place, can miss the bound.
Values may be sent and summed in bfloat16 or wider, within the bound.
No kernel may reach another device: no remote copies, remote signals or barrier semaphores. Data moves between devices by JAX's collectives and lax.ppermute only.
A program may use at most 64 MiB of HBM per device.

v0:
```python
import math

import jax
import jax.numpy as jnp
from jax import lax
from jax.sharding import PartitionSpec as P

FEAT = 128
CLASSES = 64


def sent_to_all(value, axis):
    devices = lax.axis_size(axis)
    return lax.all_to_all(
        jnp.broadcast_to(value[None], (devices, *value.shape)), axis, 0, 0, tiled=True
    )


def laid_out(parts, dim):
    parts = jnp.moveaxis(parts, 0, dim)
    lengths = parts.shape
    return parts.reshape(*lengths[:dim], lengths[dim] * lengths[dim + 1], *lengths[dim + 2 :])


def gathered_copies(value, axis, dim):
    parts = sent_to_all(value, axis)
    return laid_out(parts, dim)


def split_up(value, dim, devices):
    lengths = value.shape
    parts = value.reshape(*lengths[:dim], devices, lengths[dim] // devices, *lengths[dim + 1 :])
    return jnp.moveaxis(parts, dim, 0)


def sum_at_owner(value, axis, dim):
    parts = split_up(value, dim, lax.axis_size(axis))
    arrived = lax.all_to_all(parts, axis, split_axis=0, concat_axis=0, tiled=True)
    return arrived.sum(axis=0)


def pair_tile(left_points, right_points, right_squares):
    left_squares = jnp.sum(left_points * left_points, axis=1)
    products = lax.dot_general(
        left_points, right_points, (((1,), (1,)), ((), ())), preferred_element_type=jnp.float32
    )
    distance = left_squares[:, None] + right_squares[None, :] - 2.0 * products
    return jnp.exp(-distance / FEAT).astype(jnp.bfloat16)


def on_device(points, labels, coefficients):
    owned_rows = points.shape[0]
    row_count = lax.axis_size("row")
    col_count = lax.axis_size("col")
    total_points = owned_rows * row_count * col_count
    logit_scale = 16.0 / math.sqrt(total_points)
    column_points = gathered_copies(points, "row", 0)
    column_squares = jnp.sum(column_points * column_points, axis=1)
    kernel_tile = pair_tile(
        lax.all_gather(points, "col", axis=0, tiled=True), column_points, column_squares
    )

    def kernel_apply(current):
        rounded = current.astype(jnp.bfloat16)
        row_values = gathered_copies(rounded, "col", 0)
        return sum_at_owner(
            lax.dot_general(
                kernel_tile,
                row_values,
                (((0,), (0,)), ((), ())),
                preferred_element_type=jnp.float32,
            ),
            "row",
            0,
        )

    onehot = (labels[:, None] == jnp.arange(CLASSES, dtype=jnp.int32)[None, :]).astype(jnp.float32)
    current = coefficients
    logits = logit_scale * kernel_apply(current)
    probabilities = jax.nn.softmax(logits, axis=1)
    residual = logit_scale * (probabilities - onehot)
    current = current - kernel_apply(residual)
    return (current, probabilities)


def solution(mesh):
    return jax.shard_map(
        on_device,
        mesh=mesh,
        in_specs=(P(("row", "col"), None), P(("row", "col")), P(("row", "col"), None)),
        out_specs=(P(("row", "col"), None), P(("row", "col"), None)),
        check_vma=False,
    )
```

profile of v0, /device:TPU:16, one launch (start us, length us, event | category | flops | bytes accessed | tf_op | source)
XLA Modules:
  0.0 169.1 jit_solution(3888223382218582229)
XLA Ops:
  7.2 0.0 all-gather.2.cloned.1.call-start
  7.2 0.7 all-gather.2.cloned.1.call-update
  7.9 1.7 broadcast_in_dim.6
  9.6 5.0 %all-to-all-start = ((f32[8,128,128]{2,1,0:T(8,128)}), f32[8,128,128]{2,1,0:T(8,128)S(1)}, u32[]{:S(2)}, u32[]{:S(2)}) async-start(f32[8,128,128]{2,1,0:T(8,128)} %broadcast_in_dim.6), calls=%async_computation | async-start | bytes 1048576 | tf_op jit(solution)/shard_map/all_to_all | solution.py:14
  14.6 0.8 convert_element_type.22
  15.3 9.3 %all-to-all-done = f32[8,128,128]{2,1,0:T(8,128)S(1)} async-done(((f32[8,128,128]{2,1,0:T(8,128)}), f32[8,128,128]{2,1,0:T(8,128)S(1)}, u32[]{:S(2)}, u32[]{:S(2)}) %all-to-all-start) | async-done | bytes 524320 | tf_op jit(solution)/shard_map/all_to_all | solution.py:14
  24.7 0.9 broadcast_in_dim.7
  25.6 11.6 %all-to-all-start.1 = ((bf16[32,128,64]{1,2,0:T(8,128)(2,1)}), bf16[32,128,64]{1,2,0:T(8,128)(2,1)S(1)}, u32[]{:S(2)}, u32[]{:S(2)}) async-start(bf16[32,128,64]{1,2,0:T(8,128)(2,1)} %broadcast_in_dim.7), calls=%async_computation.1 | async-start | bytes 1048576 | tf_op jit(solution)/shard_map/all_to_all | solution.py:14
  37.2 0.2 multiply_reduce_fusion.1
  37.4 17.9 %all-to-all-done.1 = bf16[32,128,64]{1,2,0:T(8,128)(2,1)S(1)} async-done(((bf16[32,128,64]{1,2,0:T(8,128)(2,1)}), bf16[32,128,64]{1,2,0:T(8,128)(2,1)S(1)}, u32[]{:S(2)}, u32[]{:S(2)}) %all-to-all-start.1) | async-done | bytes 524320 | tf_op jit(solution)/shard_map/all_to_all | solution.py:14
  55.3 0.3 copy.7
  55.7 0.2 reshape.76
  55.9 36.3 %all-gather.2.cloned.1.call-done = f32[4096,128]{1,0:T(8,128)} async-done(((f32[128,128]{1,0:T(8,128)}), f32[4096,128]{1,0:T(8,128)}) %all-gather.2.cloned.1.call-update) | async-done | bytes 2097168 | tf_op jit(solution)/shard_map/all_gather | solution.py:60
  92.2 2.2 %multiply_reduce_fusion = f32[4096]{0:T(1024)S(1)} fusion(f32[4096,128]{1,0:T(8,128)} %all-gather.2.cloned.1.call-done), kind=kLoop, calls=%fused_computation.1 | loop fusion | flops 1044480 | bytes 2113536 | tf_op jit(solution)/shard_map/reduce_sum | solution.py:43
  94.5 6.0 %exponential_convert_fusion = bf16[1024,4096]{1,0:T(8,128)(2,1)S(1)} fusion(f32[1024,128]{1,0:T(8,128)S(1)} %bitcast.15, f32[4096,128]{1,0:T(8,128)} %all-gather.2.cloned.1.call-done, f32[1024]{0:T(1024)S(1)} %bitcast.16, f32[4096]{0:T(1024)S(1)} %multiply_reduce_fusion), kind=kOutput, calls=%fused_computation | convolution fusion | flops 1098907648 | bytes 11030528 | tf_op jit(solution)/shard_map/dot_general | solution.py:44
  100.4 0.0 copy-start
  100.4 0.0 copy-start.2
  100.4 3.2 %copy-done = bf16[1024,4096]{1,0:T(8,128)(2,1)} copy-done((bf16[1024,4096]{1,0:T(8,128)(2,1)}, bf16[1024,4096]{1,0:T(8,128)(2,1)S(1)}, u32[]{:S(2)}) %copy-start) | copy-done | bytes 8388632
  103.6 2.7 %fusion.3 = f32[8,128,64]{1,2,0:T(8,128)S(1)} fusion(bf16[8,128,4096]{2,1,0:T(8,128)(2,1)S(1)} %bitcast.13, bf16[4096,64,1]{0,1,2:T(8,128)(2,1)S(1)} %reshape.76), kind=kOutput, calls=%fused_computation.9 | convolution fusion | flops 536870912 | bytes 9175040 | tf_op jit(solution)/shard_map/dot_general | solution.py:67
  106.3 0.0 copy-start.1
  106.3 13.4 %all_to_all.25 = f32[8,128,64]{1,2,0:T(8,128)S(1)} all-to-all(f32[8,128,64]{1,2,0:T(8,128)S(1)} %fusion.3), channel_id=1, replica_groups=mesh['row'=8,'col'=32] {'row'}, dimensions={0} | all-to-all | bytes 524288 | tf_op jit(solution)/shard_map/all_to_all | solution.py:38
  119.8 0.0 copy-done.2
  119.8 0.6 multiply_convert_fusion
  120.4 0.1 broadcast_in_dim.8
  120.5 24.6 %all_to_all.26 = bf16[32,128,64]{1,2,0:T(8,128)(2,1)S(1)} all-to-all(bf16[32,128,64]{1,2,0:T(8,128)(2,1)S(1)} %broadcast_in_dim.8), channel_id=1, replica_groups=mesh['row'=8,'col'=32] {'col'}, dimensions={0} | all-to-all | bytes 1048576 | tf_op jit(solution)/shard_map/all_to_all | solution.py:14
  145.2 0.3 copy.8
  145.5 0.2 reshape.77
  145.8 6.0 %fusion.4 = f32[8,128,64]{1,2,0:T(8,128)S(1)} fusion(bf16[8,128,4096]{2,1,0:T(8,128)(2,1)} %bitcast.14, bf16[4096,64,1]{0,1,2:T(8,128)(2,1)S(1)} %reshape.77), kind=kOutput, calls=%fused_computation.10 | convolution fusion | flops 536870912 | bytes 9175040 | tf_op jit(solution)/shard_map/dot_general | solution.py:67
  151.8 9.8 %all_to_all.27 = f32[8,128,64]{1,2,0:T(8,128)S(1)} all-to-all(f32[8,128,64]{1,2,0:T(8,128)S(1)} %fusion.4), channel_id=1, replica_groups=mesh['row'=8,'col'=32] {'row'}, dimensions={0} | all-to-all | bytes 524288 | tf_op jit(solution)/shard_map/all_to_all | solution.py:38
  161.6 0.0 copy-done.1
  161.7 0.6 sub.30
  (4 shorter events, 0.1 us)
Async XLA Ops:
  7.2 85.1 %all-gather.2.cloned.1.call-start = ((), (), s32[]{:S(2)}) async-start(), calls=%async_computation.5 | async-start | bytes 2162688 | tf_op jit(solution)/shard_map/all_gather | solution.py:60
  9.6 15.1 %all-to-all-start = ((f32[8,128,128]{2,1,0:T(8,128)}), f32[8,128,128]{2,1,0:T(8,128)S(1)}, u32[]{:S(2)}, u32[]{:S(2)}) async-start(f32[8,128,128]{2,1,0:T(8,128)} %broadcast_in_dim.6), calls=%async_computation | async-start | bytes 1048576 | tf_op jit(solution)/shard_map/all_to_all | solution.py:14
  25.6 29.8 %all-to-all-start.1 = ((bf16[32,128,64]{1,2,0:T(8,128)(2,1)}), bf16[32,128,64]{1,2,0:T(8,128)(2,1)S(1)}, u32[]{:S(2)}, u32[]{:S(2)}) async-start(bf16[32,128,64]{1,2,0:T(8,128)(2,1)} %broadcast_in_dim.7), calls=%async_computation.1 | async-start | bytes 1048576 | tf_op jit(solution)/shard_map/all_to_all | solution.py:14
  100.4 3.2 %copy-start = (bf16[1024,4096]{1,0:T(8,128)(2,1)}, bf16[1024,4096]{1,0:T(8,128)(2,1)S(1)}, u32[]{:S(2)}) copy-start(bf16[1024,4096]{1,0:T(8,128)(2,1)S(1)} %exponential_convert_fusion) | copy-start | bytes 25165828
  100.4 19.4 %copy-start.2 = (s32[128]{0:T(128)S(1)}, s32[128]{0:T(128)}, u32[]{:S(2)}) copy-start(s32[128]{0:T(128)} %param.4) | copy-start | bytes 1540
  106.3 55.3 %copy-start.1 = (f32[128,64]{0,1:T(8,128)S(1)}, f32[128,64]{0,1:T(8,128)}, u32[]{:S(2)}) copy-start(f32[128,64]{0,1:T(8,128)} %param.5) | copy-start | bytes 98308
Sparse Core Ops, SparseCore 0:
  10.8 81.4 all-gather.1
where the time goes:
time: 170 us; the launch traced here: 169 us
  waiting for transfers between devices  64.3 us (38%)
  blocking collectives  47.8 us (28%)
  starting transfers between devices  16.6 us (10%)
  matrix products  14.7 us (9%)
  between operations  14.1 us (8%)
  local copies, waits for them, and re-layouts  7.04 us (4%)
  other arithmetic  4.52 us (3%)
    all_gather x1, waiting for transfers between devices, on_device(): lax.all_gather(points, 'col', axis=0, tiled=True)  36.3 us
    all_to_all x2, waiting for transfers between devices, sent_to_all(): lax.all_to_all(jnp.broadcast_to(value[None], (devices, *value.shape)), ax...  27.3 us
    all_to_all x1, blocking collectives, sent_to_all(): lax.all_to_all(jnp.broadcast_to(value[None], (devices, *value.shape)), ax...  24.6 us
    all_to_all x2, blocking collectives, sum_at_owner(): lax.all_to_all(parts, axis, split_axis=0, concat_axis=0, tiled=True)  23.2 us
    all_to_all x2, starting transfers between devices, sent_to_all(): lax.all_to_all(jnp.broadcast_to(value[None], (devices, *value.shape)), ax...  16.6 us
    dot_general x2, matrix products, kernel_apply(): lax.dot_general(kernel_tile, row_values, (((0,), (0,)), ((), ())), prefer...  8.72 us
    dot_general x1, matrix products, pair_tile(): lax.dot_general(left_points, right_points, (((1,), (1,)), ((), ())), pref...  5.96 us
  transfers between devices with their start and end apart: 3, of which 3 were waited for; matrix products, arithmetic and copies ran while one was open for 2% of the time, Pallas kernels for 0%

commit v1 on v0

v1 whole, which is shorter than its diff:
```python
import functools
import math

import jax
import jax.numpy as jnp
from jax import lax
from jax.experimental import pallas as pl
from jax.experimental.pallas import tpu as pltpu
from jax.sharding import PartitionSpec as P

FEAT = 128
CLASSES = 64
LOG2E = math.log2(math.e)
BLOCKS = 2
CHUNK = 512
BF16 = jnp.bfloat16
F32 = jnp.float32


def z_groups(cols):
    return [[z * 4 + rest for z in range(cols // 4)] for rest in range(4)]


def plane_groups(rows, cols):
    return [
        [row * cols + z * 4 + y_hi * 2 + core for row in range(rows) for y_hi in range(2)]
        for z in range(cols // 4)
        for core in range(2)
    ]


def other_core(value, cols):
    return lax.ppermute(value, "col", [(col, col ^ 1) for col in range(cols)])


def extended(block, left):
    rows = block.shape[0]
    wide = block.astype(F32)
    square = jnp.sum(wide * wide, axis=1, keepdims=True) * (-1.0 / FEAT)
    first = square.astype(BF16).astype(F32)
    rest = square - first
    second = rest.astype(BF16).astype(F32)
    third = rest - second
    lane = lax.broadcasted_iota(jnp.int32, (rows, FEAT), 1)
    at = 0 if left else 3
    ones = 3 - at
    extra = jnp.where((lane >= ones) & (lane < ones + 3), 1.0, 0.0)
    extra = jnp.where(lane == at, first, extra)
    extra = jnp.where(lane == at + 1, second, extra)
    extra = jnp.where(lane == at + 2, third, extra)
    scaled = block * jnp.asarray(2.0 / FEAT, BF16) if left else block
    return jnp.concatenate([scaled, extra.astype(BF16)], axis=1)


def tile_kernel(own, other, right, tile, sums, right_ext, total):
    step = pl.program_id(0)
    count, points = right.shape[0], right.shape[1]
    width = count * points

    @pl.when(step == 0)
    def _():
        right_ext[...] = extended(right[...].reshape(width, FEAT), False)
        total[...] = jnp.zeros_like(total)

    blocks = [ref[g] for ref in (own, other) for g in range(BLOCKS)]
    left = extended(jnp.concatenate([b[:points] for b in blocks], axis=0), True)
    values = jnp.concatenate([b[points:] for b in blocks], axis=1)
    for start in range(0, width, CHUNK):
        at = slice(start, start + CHUNK)
        exponent = lax.dot_general(
            left, right_ext[at, :], (((1,), (1,)), ((), ())), preferred_element_type=F32
        )
        kernel = jnp.exp2(exponent * LOG2E).astype(BF16)
        tile[:, at] = kernel
        total[:, at] += jnp.dot(values, kernel, preferred_element_type=F32)

    @pl.when(step == pl.num_programs(0) - 1)
    def _():
        for k in range(count):
            sums[k] = total[:, k * points : (k + 1) * points]


def tile_and_sums(own, other, right):
    blocks, packed, _ = own.shape
    count, points, _ = right.shape
    rows, width = 2 * BLOCKS * points, count * points
    left_spec = pl.BlockSpec((BLOCKS, packed, FEAT), lambda i: (i, 0, 0))
    return pl.pallas_call(
        tile_kernel,
        grid=(blocks // BLOCKS,),
        in_specs=[left_spec, left_spec, pl.BlockSpec(right.shape, lambda i: (0, 0, 0))],
        out_specs=[
            pl.BlockSpec((rows, width), lambda i: (i, 0)),
            pl.BlockSpec((count, CLASSES, points), lambda i: (0, 0, 0)),
        ],
        out_shape=[
            jax.ShapeDtypeStruct((2 * blocks * points, width), BF16),
            jax.ShapeDtypeStruct((count, CLASSES, points), F32),
        ],
        scratch_shapes=[pltpu.VMEM((width, 2 * FEAT), BF16), pltpu.VMEM((CLASSES, width), F32)],
        compiler_params=pltpu.CompilerParams(vmem_limit_bytes=32 << 20),
        name="tile_and_sums",
    )(own, other, right)


def apply_kernel(own, other, tile, sums, total):
    step = pl.program_id(0)
    count, _, points = sums.shape

    @pl.when(step == 0)
    def _():
        total[...] = jnp.zeros_like(total)

    values = jnp.concatenate([ref[g] for ref in (own, other) for g in range(BLOCKS)], axis=1)
    total[...] += jnp.dot(values, tile[...], preferred_element_type=F32)

    @pl.when(step == pl.num_programs(0) - 1)
    def _():
        for k in range(count):
            sums[k] = total[:, k * points : (k + 1) * points]


def apply_tile(own, other, tile, count):
    blocks, _, points = own.shape
    rows, width = 2 * BLOCKS * points, tile.shape[1]
    left_spec = pl.BlockSpec((BLOCKS, CLASSES, points), lambda i: (i, 0, 0))
    return pl.pallas_call(
        apply_kernel,
        grid=(blocks // BLOCKS,),
        in_specs=[left_spec, left_spec, pl.BlockSpec((rows, width), lambda i: (i, 0))],
        out_specs=pl.BlockSpec((count, CLASSES, points), lambda i: (0, 0, 0)),
        out_shape=jax.ShapeDtypeStruct((count, CLASSES, points), F32),
        scratch_shapes=[pltpu.VMEM((CLASSES, width), F32)],
        compiler_params=pltpu.CompilerParams(vmem_limit_bytes=32 << 20),
        name="apply_tile",
    )(own, other, tile)


def on_device(rows, cols, points, labels, coefficients):
    total_points = points.shape[0] * rows * cols
    logit_scale = 16.0 / math.sqrt(total_points)
    in_z, in_plane = z_groups(cols), plane_groups(rows, cols)
    zs, planes = len(in_z[0]), len(in_plane[0])

    def along_z(value):
        copies = jnp.broadcast_to(value[None], (zs, *value.shape))
        return lax.all_to_all(copies, "col", 0, 0, tiled=True, axis_index_groups=in_z)

    def in_the_plane(parts):
        return lax.all_to_all(
            parts, ("row", "col"), 0, 0, tiled=True, axis_index_groups=in_plane
        )

    current = coefficients.T
    near = points.astype(BF16)
    own = along_z(jnp.concatenate([near, current.astype(BF16)], axis=0))
    other = other_core(own, cols)
    right = in_the_plane(jnp.broadcast_to(near[None], (planes, *near.shape)))
    tile, sums = tile_and_sums(own, other, right)
    logits = logit_scale * in_the_plane(sums).sum(axis=0)
    probabilities = jax.nn.softmax(logits, axis=0)
    classes = jnp.arange(CLASSES, dtype=jnp.int32)
    onehot = (labels[None, :] == classes[:, None]).astype(F32)
    residual = logit_scale * (probabilities - onehot)
    own = along_z(residual.astype(BF16))
    sums = apply_tile(own, other_core(own, cols), tile, planes)
    current = current - in_the_plane(sums).sum(axis=0)
    return current.T, probabilities.T


def solution(mesh):
    rows, cols = mesh.shape["row"], mesh.shape["col"]
    return jax.shard_map(
        functools.partial(on_device, rows, cols),
        mesh=mesh,
        in_specs=(P(("row", "col"), None), P(("row", "col")), P(("row", "col"), None)),
        out_specs=(P(("row", "col"), None), P(("row", "col"), None)),
        check_vma=False,
    )
```

time: 170 us -> 103 us (0.61)
  waiting for transfers between devices: 64.3 us -> 9.18 us
  blocking collectives: 47.8 us -> 63.5 us
  matrix products: 14.7 us -> 0 us
  between operations: 14.1 us -> 0.7 us
  starting transfers between devices: 16.6 us -> 7.28 us
  Pallas kernels: 0 us -> 9 us
    all_gather x1 -> x0, waiting for transfers between devices: 36.3 us -> none  [on_device(): lax.all_gather(points, 'col', axis=0, tiled=True)]
    all_to_all x2 -> x1, waiting for transfers between devices: 27.3 us -> 7.83 us  [in_the_plane(): lax.all_to_all(parts, ('row', 'col'), 0, 0, tiled=True, axis_index_groups...]
    all_to_all x3 -> x4, blocking collectives: 47.8 us -> 63.5 us  [the longest x2 35.2 us: along_z(): lax.all_to_all(copies, 'col', 0, 0, tiled=True, axis_index_groups=in_z)]
    dot_general x3 -> x0, matrix products: 14.7 us -> none  [the longest x2 8.72 us: kernel_apply(): lax.dot_general(kernel_tile, row_values, (((0,), (0,)), ((), ())), prefer...]
    all_to_all x2 -> x1, starting transfers between devices: 16.6 us -> 7.28 us  [in_the_plane(): lax.all_to_all(parts, ('row', 'col'), 0, 0, tiled=True, axis_index_groups...]
    pallas_call x0 -> x2, Pallas kernels: none -> 9 us  [the longest x1 6.96 us: tile_and_sums(): pl.pallas_call(tile_kernel, grid=(blocks // BLOCKS,), in_specs=[left_spec...]
    unnamed x6, local copies, waits for them, and re-layouts: 3.21 us -> 6.6 us
    reduce_sum x5 -> x3, other arithmetic: 2.48 us -> 0.1 us  [the longest x1 0.03 us: on_device(): current = current - in_the_plane(sums).sum(axis=0)]
  transfers between devices with their start and end apart: 3 -> 3, of which waited for: 3 -> 2; matrix products, arithmetic and copies ran while one was open for 2% -> 0% of each run, Pallas kernels for 0% -> 0%
where the time goes in v1:
time: 103 us; the launch traced here: 101 us
  blocking collectives  63.5 us (62%)
  waiting for transfers between devices  9.18 us (9%)
  Pallas kernels  9 us (9%)
  local copies, waits for them, and re-layouts  7.56 us (7%)
  starting transfers between devices  7.28 us (7%)
  other arithmetic  3.65 us (4%)
    all_to_all x2, blocking collectives, along_z(): lax.all_to_all(copies, 'col', 0, 0, tiled=True, axis_index_groups=in_z)  35.2 us
    all_to_all x2, blocking collectives, in_the_plane(): lax.all_to_all(parts, ('row', 'col'), 0, 0, tiled=True, axis_index_groups...  28.4 us
    all_to_all x1, waiting for transfers between devices, in_the_plane(): lax.all_to_all(parts, ('row', 'col'), 0, 0, tiled=True, axis_index_groups...  7.83 us
    all_to_all x1, starting transfers between devices, in_the_plane(): lax.all_to_all(parts, ('row', 'col'), 0, 0, tiled=True, axis_index_groups...  7.28 us
    pallas_call x1, Pallas kernels, tile_and_sums(): pl.pallas_call(tile_kernel, grid=(blocks // BLOCKS,), in_specs=[left_spec...  6.96 us
    unnamed x6, local copies, waits for them, and re-layouts  6.6 us
  transfers between devices with their start and end apart: 3, of which 2 were waited for; matrix products, arithmetic and copies ran while one was open for 0% of the time, Pallas kernels for 0%

profile of v1, /device:TPU:16, one launch (start us, length us, event | category | flops | bytes accessed | tf_op | source)
XLA Modules:
  0.0 100.9 jit_solution(7936783218621801729)
XLA Ops:
  0.6 0.8 convert_bitcast_fusion
  1.4 0.8 convert_element_type.23
  2.2 0.1 broadcast_in_dim.6
  2.3 0.0 copy-start.2
  2.3 22.9 %all_to_all.25.own = bf16[8,192,128]{2,1,0:T(8,128)(2,1)S(1)} all-to-all(bf16[8,192,128]{2,1,0:T(8,128)(2,1)S(1)} %broadcast_in_dim.6), channel_id=1, replica_groups={{0,4,8,12,16,20,24,28},{1,5,9,13,17,21,25,29},{2,6,10,14,18,22,26,30},{..., dimensions={0} | all-to-all | bytes 786432 | tf_op jit(solution)/shard_map/all_to_all | solution.py:147
  25.3 0.9 broadcast_in_dim.7
  26.2 7.3 %all-to-all-start.1 = ((bf16[16,128,128]{2,1,0:T(8,128)(2,1)}), bf16[16,128,128]{2,1,0:T(8,128)(2,1)S(1)}, u32[]{:S(2)}, u32[]{:S(2)}) async-start(bf16[16,128,128]{2,1,0:T(8,128)(2,1)} %broadcast_in_dim.7), calls=%async_computation.1 | async-start | bytes 1048576 | tf_op jit(solution)/shard_map/all_to_all | solution.py:150
  33.4 0.0 collective-permute-start
  33.4 7.8 %all-to-all-done.1.right = bf16[16,128,128]{2,1,0:T(8,128)(2,1)S(1)} async-done(((bf16[16,128,128]{2,1,0:T(8,128)(2,1)}), bf16[16,128,128]{2,1,0:T(8,128)(2,1)S(1)}, u32[]{:S(2)}, u32[]{:S(2)}) %all-to-all-start.1) | async-done | bytes 524320 | tf_op jit(solution)/shard_map/all_to_all | solution.py:150
  41.3 0.0 collective-permute-done.other
  41.3 7.0 %tile_and_sums.1 = (bf16[2048,2048]{1,0:T(8,128)(2,1)S(1)}, f32[16,64,128]{2,1,0:T(8,128)S(1)}) custom-call(bf16[8,192,128]{2,1,0:T(8,128)(2,1)S(1)} %all_to_all.25.own, bf16[8,192,128]{2,1,0:T(8,128)(2,1)S(1)} %collective-permute-done.other, bf16[16,128,128]{2,1,0:T(8,128)(2,1)S(1)} %all-to-all-done.1.right), custom_call_target="tpu_custom_call" | custom-call | tf_op jit(solution)/shard_map/tile_and_sums/pallas_call | solution.py:88
  48.3 0.0 copy-start
  48.3 3.2 %copy-done = bf16[2048,2048]{1,0:T(8,128)(2,1)} copy-done((bf16[2048,2048]{1,0:T(8,128)(2,1)}, bf16[2048,2048]{1,0:T(8,128)(2,1)S(1)}, u32[]{:S(2)}) %copy-start) | copy-done | bytes 8388632
  51.5 13.3 %all_to_all.26 = f32[16,64,128]{2,1,0:T(8,128)S(1)} all-to-all(f32[16,64,128]{2,1,0:T(8,128)S(1)} %get-tuple-element.4), channel_id=1, replica_groups={{0,2,32,34,64,66,96,98,128,130,160,162,192,194,224,226},{1,3,33,35,65,6..., dimensions={0} | all-to-all | bytes 1048576 | tf_op jit(solution)/shard_map/all_to_all | solution.py:150
  64.9 1.3 %fusion.2 = (f32[128,64]{0,1:T(8,128)}, bf16[64,128]{1,0:T(8,128)(2,1)S(1)}) fusion(f32[128]{0:T(128)S(1)} %fusion.1, f32[128]{0:T(128)S(1)} %multiply_reduce_fusion, f32[64,128]{1,0:T(8,128)S(1)} %reduce_sum.29, s32[128]{0:T(128)} %param.4), kind=kLoop, calls=%fused_computation.9 | loop fusion | flops 65536 | bytes 83456 | tf_op jit(solution)/shard_map/div | solution.py:161
  66.2 12.2 %all_to_all.27.own = bf16[8,64,128]{2,1,0:T(8,128)(2,1)S(1)} all-to-all(bf16[8,64,128]{2,1,0:T(8,128)(2,1)S(1)} %broadcast_in_dim.8), channel_id=1, replica_groups={{0,4,8,12,16,20,24,28},{1,5,9,13,17,21,25,29},{2,6,10,14,18,22,26,30},{..., dimensions={0} | all-to-all | bytes 262144 | tf_op jit(solution)/shard_map/all_to_all | solution.py:147
  78.4 0.0 collective-permute-start.1
  78.4 1.3 %collective-permute-done.1.other = bf16[8,64,128]{2,1,0:T(8,128)(2,1)S(1)} collective-permute-done((bf16[8,64,128]{2,1,0:T(8,128)(2,1)S(1)}, bf16[8,64,128]{2,1,0:T(8,128)(2,1)S(1)}, u32[]{:S(2)}, u32[]{:S(2)}) %collective-permute-start.1) | collective-permute-done | bytes 131104 | tf_op jit(solution)/shard_map/ppermute | solution.py:33
  79.8 0.0 copy-start.1
  79.8 3.4 %copy-done.1 = bf16[2048,2048]{1,0:T(8,128)(2,1)S(1)} copy-done((bf16[2048,2048]{1,0:T(8,128)(2,1)S(1)}, bf16[2048,2048]{1,0:T(8,128)(2,1)}, u32[]{:S(2)}) %copy-start.1) | copy-done | bytes 8388632
  83.1 2.0 %apply_tile.1 = f32[16,64,128]{2,1,0:T(8,128)S(1)} custom-call(bf16[8,64,128]{2,1,0:T(8,128)(2,1)S(1)} %all_to_all.27.own, bf16[8,64,128]{2,1,0:T(8,128)(2,1)S(1)} %collective-permute-done.1.other, bf16[2048,2048]{1,0:T(8,128)(2,1)S(1)} %copy-done.1), custom_call_target="tpu_custom_call" | custom-call | tf_op jit(solution)/shard_map/apply_tile/pallas_call | solution.py:127
  85.2 15.1 %all_to_all.28 = f32[16,64,128]{2,1,0:T(8,128)S(1)} all-to-all(f32[16,64,128]{2,1,0:T(8,128)S(1)} %apply_tile.1), channel_id=1, replica_groups={{0,2,32,34,64,66,96,98,128,130,160,162,192,194,224,226},{1,3,33,35,65,6..., dimensions={0} | all-to-all | bytes 1048576 | tf_op jit(solution)/shard_map/all_to_all | solution.py:150
  100.3 0.0 copy-done.2
  100.3 0.6 bitcast_subtract_fusion
  (6 shorter events, 0.2 us)
Async XLA Ops:
  2.3 98.0 %copy-start.2 = (f32[128,64]{0,1:T(8,128)S(1)}, f32[128,64]{0,1:T(8,128)}, u32[]{:S(2)}) copy-start(f32[128,64]{0,1:T(8,128)} %param.5) | copy-start | bytes 98308
  26.2 15.1 %all-to-all-start.1 = ((bf16[16,128,128]{2,1,0:T(8,128)(2,1)}), bf16[16,128,128]{2,1,0:T(8,128)(2,1)S(1)}, u32[]{:S(2)}, u32[]{:S(2)}) async-start(bf16[16,128,128]{2,1,0:T(8,128)(2,1)} %broadcast_in_dim.7), calls=%async_computation.1 | async-start | bytes 1048576 | tf_op jit(solution)/shard_map/all_to_all | solution.py:150
  33.4 7.8 %collective-permute-start = (bf16[8,192,128]{2,1,0:T(8,128)(2,1)S(1)}, bf16[8,192,128]{2,1,0:T(8,128)(2,1)S(1)}, u32[]{:S(2)}, u32[]{:S(2)}) collective-permute-start(bf16[8,192,128]{2,1,0:T(8,128)(2,1)S(1)} %all_to_all.25.own), channel_id=1, source_target_pairs={{0,1},{1,0},{2,3},{3,2},{4,5},{5,4},{6,7},{7,6},{8,9},{9,8},{10,11... | collective-permute-start | bytes 1179656 | tf_op jit(solution)/shard_map/ppermute | solution.py:33
  48.3 3.2 %copy-start = (bf16[2048,2048]{1,0:T(8,128)(2,1)}, bf16[2048,2048]{1,0:T(8,128)(2,1)S(1)}, u32[]{:S(2)}) copy-start(bf16[2048,2048]{1,0:T(8,128)(2,1)S(1)} %get-tuple-element.5.tile) | copy-start | bytes 25165828
  78.4 1.3 %collective-permute-start.1 = (bf16[8,64,128]{2,1,0:T(8,128)(2,1)S(1)}, bf16[8,64,128]{2,1,0:T(8,128)(2,1)S(1)}, u32[]{:S(2)}, u32[]{:S(2)}) collective-permute-start(bf16[8,64,128]{2,1,0:T(8,128)(2,1)S(1)} %all_to_all.27.own), channel_id=1, source_target_pairs={{0,1},{1,0},{2,3},{3,2},{4,5},{5,4},{6,7},{7,6},{8,9},{9,8},{10,11... | collective-permute-start | bytes 393224 | tf_op jit(solution)/shard_map/ppermute | solution.py:33
  79.8 3.4 %copy-start.1 = (bf16[2048,2048]{1,0:T(8,128)(2,1)S(1)}, bf16[2048,2048]{1,0:T(8,128)(2,1)}, u32[]{:S(2)}) copy-start(bf16[2048,2048]{1,0:T(8,128)(2,1)} %copy-done) | copy-start | bytes 25165828

commit v2 on v1

v2 whole, which is shorter than its diff:
```python
import functools
import math

import jax
import jax.numpy as jnp
from jax import lax
from jax.experimental import pallas as pl
from jax.experimental.pallas import tpu as pltpu
from jax.sharding import PartitionSpec as P


FEAT = 128
CLASSES = 64
LOG2E = math.log2(math.e)
ROWS = 1024
CHUNK = 512
BF16 = jnp.bfloat16
F32 = jnp.float32


def z_groups(cols):
    return [[z * 4 + rest for z in range(cols // 4)] for rest in range(4)]


def plane_groups(rows, cols):
    return [
        [row * cols + z * 4 + y_hi * 2 + core for row in range(rows) for y_hi in range(2)]
        for z in range(cols // 4)
        for core in range(2)
    ]


def other_core(value, cols):
    return lax.ppermute(value, "col", [(col, col ^ 1) for col in range(cols)])


def extended(block, left):
    rows = block.shape[0]
    wide = block.astype(F32)
    square = jnp.sum(wide * wide, axis=1, keepdims=True) * (-1.0 / FEAT)
    first = square.astype(BF16).astype(F32)
    second = square - first
    lane = lax.broadcasted_iota(jnp.int32, (rows, FEAT), 1)
    at = 0 if left else 2
    ones = 2 - at
    extra = jnp.where((lane >= ones) & (lane < ones + 2), 1.0, 0.0)
    extra = jnp.where(lane == at, first, extra)
    extra = jnp.where(lane == at + 1, second, extra)
    scaled = block * jnp.asarray(2.0 / FEAT, BF16) if left else block
    return jnp.concatenate([scaled, extra.astype(BF16)], axis=1)


def build_tile(packed, right_ext, tile):
    points, width = packed.shape[1] - CLASSES, tile.shape[1]
    per_step = ROWS // points
    for step in range(packed.shape[0] // per_step):
        blocks = range(step * per_step, (step + 1) * per_step)
        left = jnp.concatenate([extended(packed[g, :points, :], True) for g in blocks], axis=0)
        for start in range(0, width, CHUNK):
            exponent = lax.dot_general(
                left,
                right_ext[start : start + CHUNK, :],
                (((1,), (1,)), ((), ())),
                preferred_element_type=F32,
            )
            tile[step * ROWS : (step + 1) * ROWS, start : start + CHUNK] = jnp.exp2(
                exponent * LOG2E
            ).astype(BF16)


def side_by_side(values):
    return jnp.concatenate([values[g] for g in range(values.shape[0])], axis=1)


def own_kernel(own, right, tile, right_ext):
    count, points, _ = right.shape
    for k in range(count):
        right_ext[k * points : (k + 1) * points, :] = extended(right[k], False)
    build_tile(own, right_ext, tile)


def other_kernel(own, own_tile, other, right_ext, tile, sums):
    count, _, points = sums.shape
    build_tile(other, right_ext, tile)
    rows = other.shape[1] - CLASSES
    total = jnp.dot(
        side_by_side(own[:, rows:, :]), own_tile[...], preferred_element_type=F32
    ) + jnp.dot(side_by_side(other[:, rows:, :]), tile[...], preferred_element_type=F32)
    for k in range(count):
        sums[k] = total[:, k * points : (k + 1) * points]


def tile_from_own(own, right):
    blocks, _, _ = own.shape
    count, points, _ = right.shape
    rows, width = blocks * points, count * points
    return pl.pallas_call(
        own_kernel,
        out_shape=[
            jax.ShapeDtypeStruct((rows, width), BF16),
            jax.ShapeDtypeStruct((width, 2 * FEAT), BF16),
        ],
        compiler_params=pltpu.CompilerParams(vmem_limit_bytes=16 << 20),
        cost_estimate=pl.CostEstimate(
            flops=4 * rows * width * FEAT, bytes_accessed=0, transcendentals=rows * width
        ),
        name="tile_from_own",
    )(own, right)


def tile_from_other(own, own_tile, other, right_ext, count):
    rows, width = own_tile.shape
    return pl.pallas_call(
        other_kernel,
        out_shape=[
            jax.ShapeDtypeStruct((rows, width), BF16),
            jax.ShapeDtypeStruct((count, CLASSES, width // count), F32),
        ],
        compiler_params=pltpu.CompilerParams(vmem_limit_bytes=16 << 20),
        name="tile_from_other",
    )(own, own_tile, other, right_ext)


def apply_kernel(own, own_tile, other, other_tile, sums):
    count, _, points = sums.shape
    total = jnp.dot(side_by_side(own), own_tile[...], preferred_element_type=F32) + jnp.dot(
        side_by_side(other), other_tile[...], preferred_element_type=F32
    )
    for k in range(count):
        sums[k] = total[:, k * points : (k + 1) * points]


def apply_tiles(own, own_tile, other, other_tile, count):
    points = own_tile.shape[1] // count
    return pl.pallas_call(
        apply_kernel,
        out_shape=jax.ShapeDtypeStruct((count, CLASSES, points), F32),
        compiler_params=pltpu.CompilerParams(vmem_limit_bytes=16 << 20),
        name="apply_tiles",
    )(own, own_tile, other, other_tile)


def pack_kernel(points, current, labels, packed, near, kept, kept_labels, wide, sems):
    rows = points.shape[0]
    copies = [
        pltpu.make_async_copy(source, target, sems.at[k])
        for k, (source, target) in enumerate(
            ((points, wide), (current, kept), (labels, kept_labels))
        )
    ]
    for copy in copies:
        copy.start()
    copies[0].wait()
    narrow = wide[...].astype(BF16)
    for k in range(near.shape[0]):
        near[k] = narrow
    for k in range(packed.shape[0]):
        packed[k, :rows] = narrow
    copies[1].wait()
    values = kept[...].astype(BF16)
    for k in range(packed.shape[0]):
        packed[k, rows:] = values
    copies[2].wait()


def pack(points, current, labels, zs, planes):
    rows = points.shape[0]
    in_hbm = pl.BlockSpec(memory_space=pltpu.HBM)
    in_vmem = pl.BlockSpec(memory_space=pltpu.VMEM)
    return pl.pallas_call(
        pack_kernel,
        in_specs=[in_hbm] * 3,
        out_specs=[in_vmem] * 4,
        out_shape=[
            jax.ShapeDtypeStruct((zs, rows + CLASSES, FEAT), BF16),
            jax.ShapeDtypeStruct((planes, rows, FEAT), BF16),
            jax.ShapeDtypeStruct(current.shape, F32),
            jax.ShapeDtypeStruct(labels.shape, jnp.int32),
        ],
        scratch_shapes=[pltpu.VMEM(points.shape, F32), pltpu.SemaphoreType.DMA((3,))],
        compiler_params=pltpu.CompilerParams(vmem_limit_bytes=8 << 20),
        name="pack",
    )(*(pltpu.with_memory_space_constraint(v, pltpu.HBM) for v in (points, current, labels)))


def softmax_kernel(logit_scale, parts, labels, residual, probabilities):
    logits = logit_scale * jnp.sum(parts[...], axis=0)
    raised = jnp.exp(logits - jnp.max(logits, axis=0, keepdims=True))
    value = raised / jnp.sum(raised, axis=0, keepdims=True)
    classes = lax.broadcasted_iota(jnp.int32, value.shape, 0)
    onehot = jnp.where(classes == labels[...], 1.0, 0.0)
    change = (logit_scale * (value - onehot)).astype(BF16)
    probabilities[...] = value
    for k in range(residual.shape[0]):
        residual[k] = change


def softmax_and_residual(parts, labels, logit_scale, zs):
    _, classes, points = parts.shape
    return pl.pallas_call(
        functools.partial(softmax_kernel, logit_scale),
        out_shape=[
            jax.ShapeDtypeStruct((zs, classes, points), BF16),
            jax.ShapeDtypeStruct((classes, points), F32),
        ],
        compiler_params=pltpu.CompilerParams(vmem_limit_bytes=8 << 20),
        name="softmax_and_residual",
    )(parts, labels)


def finish_kernel(parts, current, probabilities, new_current, out_probabilities):
    new_current[...] = current[...] - jnp.sum(parts[...], axis=0)
    out_probabilities[...] = probabilities[...]


def finish(parts, current, probabilities):
    shape = jax.ShapeDtypeStruct(current.shape, F32)
    return pl.pallas_call(
        finish_kernel,
        out_shape=[shape, shape],
        compiler_params=pltpu.CompilerParams(vmem_limit_bytes=8 << 20),
        name="finish",
    )(parts, current, probabilities)


def on_device(rows, cols, points, labels, coefficients):
    total_points = points.shape[0] * rows * cols
    logit_scale = 16.0 / math.sqrt(total_points)
    in_z, in_plane = z_groups(cols), plane_groups(rows, cols)
    zs, planes = len(in_z[0]), len(in_plane[0])

    def along_z(parts):
        return lax.all_to_all(parts, "col", 0, 0, tiled=True, axis_index_groups=in_z)

    def in_the_plane(parts):
        return lax.all_to_all(
            parts, ("row", "col"), 0, 0, tiled=True, axis_index_groups=in_plane
        )

    current = coefficients.T
    packed, near, current, labels = pack(points, current, labels[None, :], zs, planes)
    right = in_the_plane(near)
    own = along_z(packed)
    other = other_core(own, cols)
    own_tile, right_ext = tile_from_own(own, right)
    other_tile, sums = tile_from_other(own, own_tile, other, right_ext, planes)
    residual, probabilities = softmax_and_residual(
        in_the_plane(sums), labels, logit_scale, zs
    )
    own = along_z(residual)
    sums = apply_tiles(own, own_tile, other_core(own, cols), other_tile, planes)
    current, probabilities = finish(in_the_plane(sums), current, probabilities)
    return current.T, probabilities.T


def solution(mesh):
    rows, cols = mesh.shape["row"], mesh.shape["col"]
    return jax.shard_map(
        functools.partial(on_device, rows, cols),
        mesh=mesh,
        in_specs=(P(("row", "col"), None), P(("row", "col")), P(("row", "col"), None)),
        out_specs=(P(("row", "col"), None), P(("row", "col"), None)),
        check_vma=False,
    )
```

time: 103 us -> 90.9 us (0.88)
  local copies, waits for them, and re-layouts: 7.56 us -> 0 us
  other arithmetic: 3.65 us -> 0 us
    unnamed x6 -> x0, local copies, waits for them, and re-layouts: 6.6 us -> none
    convert_element_type x2 -> x0, other arithmetic: 1.61 us -> none  [the longest x1 0.84 us: on_device(): near = points.astype(BF16)]
    div x1 -> x0, other arithmetic: 1.29 us -> none  [on_device(): probabilities = jax.nn.softmax(logits, axis=0)]
    pallas_call x2 -> x6, Pallas kernels: 9 us -> 8.38 us  [the longest x1 2.75 us: tile_from_other(): pl.pallas_call(other_kernel, out_shape=[jax.ShapeDtypeStruct((rows, width...]
  transfers between devices with their start and end apart: 3 -> 3, of which waited for: 2 -> 2; matrix products, arithmetic and copies ran while one was open for 0% -> 0% of each run, Pallas kernels for 0% -> 2%
where the time goes in v2:
time: 90.9 us; the launch traced here: 89.1 us
  blocking collectives  63.6 us (70%)
  waiting for transfers between devices  9.18 us (10%)
  Pallas kernels  8.38 us (9%)
  starting transfers between devices  7.28 us (8%)
    all_to_all x2, blocking collectives, along_z(): lax.all_to_all(parts, 'col', 0, 0, tiled=True, axis_index_groups=in_z)  35.2 us
    all_to_all x2, blocking collectives, in_the_plane(): lax.all_to_all(parts, ('row', 'col'), 0, 0, tiled=True, axis_index_groups...  28.4 us
    all_to_all x1, waiting for transfers between devices, in_the_plane(): lax.all_to_all(parts, ('row', 'col'), 0, 0, tiled=True, axis_index_groups...  7.83 us
    all_to_all x1, starting transfers between devices, in_the_plane(): lax.all_to_all(parts, ('row', 'col'), 0, 0, tiled=True, axis_index_groups...  7.28 us
    pallas_call x1, Pallas kernels, tile_from_other(): pl.pallas_call(other_kernel, out_shape=[jax.ShapeDtypeStruct((rows, width...  2.75 us
  transfers between devices with their start and end apart: 3, of which 2 were waited for; matrix products, arithmetic and copies ran while one was open for 0% of the time, Pallas kernels for 2%

profile of v2, /device:TPU:16, one launch (start us, length us, event | category | flops | bytes accessed | tf_op | source)
XLA Modules:
  0.0 89.1 jit_solution(11637412818931577044)
XLA Ops:
  0.6 1.8 %pack.1 = (bf16[8,192,128]{2,1,0:T(8,128)(2,1)S(1)}, bf16[16,128,128]{2,1,0:T(8,128)(2,1)}, f32[64,128]{1,0:T(8,128)S(1)}, s32[1,128]{1,0:T(1,128)S(1)}) custom-call(f32[128,128]{1,0:T(8,128)} %points.1, f32[64,128]{1,0:T(8,128)} %bitcast.4, s32[1,128]{1,0:T(1,128)} %bitcast.5), custom_call_target="tpu_custom_call" | custom-call | tf_op jit(solution)/shard_map/pack/pallas_call | solution.py:170
  2.4 22.9 %all_to_all.25.own = bf16[8,192,128]{2,1,0:T(8,128)(2,1)S(1)} all-to-all(bf16[8,192,128]{2,1,0:T(8,128)(2,1)S(1)} %get-tuple-element.14), channel_id=1, replica_groups={{0,4,8,12,16,20,24,28},{1,5,9,13,17,21,25,29},{2,6,10,14,18,22,26,30},{..., dimensions={0} | all-to-all | bytes 786432 | tf_op jit(solution)/shard_map/all_to_all | solution.py:233
  25.4 7.3 %all-to-all-start.1 = ((bf16[16,128,128]{2,1,0:T(8,128)(2,1)}), bf16[16,128,128]{2,1,0:T(8,128)(2,1)S(1)}, u32[]{:S(2)}, u32[]{:S(2)}) async-start(bf16[16,128,128]{2,1,0:T(8,128)(2,1)} %get-tuple-element.15), calls=%async_computation.1 | async-start | bytes 1048576 | tf_op jit(solution)/shard_map/all_to_all | solution.py:236
  32.6 0.0 collective-permute-start
  32.6 7.8 %all-to-all-done.1.right = bf16[16,128,128]{2,1,0:T(8,128)(2,1)S(1)} async-done(((bf16[16,128,128]{2,1,0:T(8,128)(2,1)}), bf16[16,128,128]{2,1,0:T(8,128)(2,1)S(1)}, u32[]{:S(2)}, u32[]{:S(2)}) %all-to-all-start.1) | async-done | bytes 524320 | tf_op jit(solution)/shard_map/all_to_all | solution.py:236
  40.5 1.6 %tile_from_own.1 = (bf16[1024,2048]{1,0:T(8,128)(2,1)S(1)}, bf16[2048,256]{1,0:T(8,128)(2,1)S(1)}) custom-call(bf16[8,192,128]{2,1,0:T(8,128)(2,1)S(1)} %all_to_all.25.own, bf16[16,128,128]{2,1,0:T(8,128)(2,1)S(1)} %all-to-all-done.1.right), custom_call_target="tpu_custom_call" | custom-call | flops 1073741824 | tf_op jit(solution)/shard_map/tile_from_own/pallas_call | solution.py:97
  42.1 0.0 collective-permute-done.other
  42.1 2.8 %tile_from_other.1 = (bf16[1024,2048]{1,0:T(8,128)(2,1)S(1)}, f32[16,64,128]{2,1,0:T(8,128)S(1)}) custom-call(bf16[8,192,128]{2,1,0:T(8,128)(2,1)S(1)} %all_to_all.25.own, bf16[1024,2048]{1,0:T(8,128)(2,1)S(1)} %get-tuple-element.16.own_tile, bf16[8,192,128]{2,1,0:T(8,128)(2,1)S(1)} %collective-permute-done.other, ...), custom_call_target="tpu_custom_call" | custom-call | tf_op jit(solution)/shard_map/tile_from_other/pallas_call | solution.py:113
  44.8 13.3 %all_to_all.26.parts = f32[16,64,128]{2,1,0:T(8,128)S(1)} all-to-all(f32[16,64,128]{2,1,0:T(8,128)S(1)} %get-tuple-element.18), channel_id=1, replica_groups={{0,2,32,34,64,66,96,98,128,130,160,162,192,194,224,226},{1,3,33,35,65,6..., dimensions={0} | all-to-all | bytes 1048576 | tf_op jit(solution)/shard_map/all_to_all | solution.py:236
  58.2 0.1 softmax_and_residual.1
  58.3 12.2 %all_to_all.27.own = bf16[8,64,128]{2,1,0:T(8,128)(2,1)S(1)} all-to-all(bf16[8,64,128]{2,1,0:T(8,128)(2,1)S(1)} %get-tuple-element.20), channel_id=1, replica_groups={{0,4,8,12,16,20,24,28},{1,5,9,13,17,21,25,29},{2,6,10,14,18,22,26,30},{..., dimensions={0} | all-to-all | bytes 262144 | tf_op jit(solution)/shard_map/all_to_all | solution.py:233
  70.5 0.0 collective-permute-start.1
  70.5 1.3 %collective-permute-done.1.other = bf16[8,64,128]{2,1,0:T(8,128)(2,1)S(1)} collective-permute-done((bf16[8,64,128]{2,1,0:T(8,128)(2,1)S(1)}, bf16[8,64,128]{2,1,0:T(8,128)(2,1)S(1)}, u32[]{:S(2)}, u32[]{:S(2)}) %collective-permute-start.1) | collective-permute-done | bytes 131104 | tf_op jit(solution)/shard_map/ppermute | solution.py:34
  71.8 1.6 %apply_tiles.1 = f32[16,64,128]{2,1,0:T(8,128)S(1)} custom-call(bf16[8,64,128]{2,1,0:T(8,128)(2,1)S(1)} %all_to_all.27.own, bf16[1024,2048]{1,0:T(8,128)(2,1)S(1)} %get-tuple-element.16.own_tile, bf16[8,64,128]{2,1,0:T(8,128)(2,1)S(1)} %collective-permute-done.1.other, bf16[1024,2048]{1,0:T(8,128)(2,1)S(1)} %get-tuple-element.21.other_tile), custom_call_target="tpu_custom_call" | custom-call | tf_op jit(solution)/shard_map/apply_tiles/pallas_call | solution.py:135
  73.4 15.1 %all_to_all.28.parts = f32[16,64,128]{2,1,0:T(8,128)S(1)} all-to-all(f32[16,64,128]{2,1,0:T(8,128)S(1)} %apply_tiles.1), channel_id=1, replica_groups={{0,2,32,34,64,66,96,98,128,130,160,162,192,194,224,226},{1,3,33,35,65,6..., dimensions={0} | all-to-all | bytes 1048576 | tf_op jit(solution)/shard_map/all_to_all | solution.py:236
  88.4 0.7 finish.1
Async XLA Ops:
  25.4 15.1 %all-to-all-start.1 = ((bf16[16,128,128]{2,1,0:T(8,128)(2,1)}), bf16[16,128,128]{2,1,0:T(8,128)(2,1)S(1)}, u32[]{:S(2)}, u32[]{:S(2)}) async-start(bf16[16,128,128]{2,1,0:T(8,128)(2,1)} %get-tuple-element.15), calls=%async_computation.1 | async-start | bytes 1048576 | tf_op jit(solution)/shard_map/all_to_all | solution.py:236
  32.6 9.4 %collective-permute-start = (bf16[8,192,128]{2,1,0:T(8,128)(2,1)S(1)}, bf16[8,192,128]{2,1,0:T(8,128)(2,1)S(1)}, u32[]{:S(2)}, u32[]{:S(2)}) collective-permute-start(bf16[8,192,128]{2,1,0:T(8,128)(2,1)S(1)} %all_to_all.25.own), channel_id=1, source_target_pairs={{0,1},{1,0},{2,3},{3,2},{4,5},{5,4},{6,7},{7,6},{8,9},{9,8},{10,11... | collective-permute-start | bytes 1179656 | tf_op jit(solution)/shard_map/ppermute | solution.py:34
  70.5 1.3 %collective-permute-start.1 = (bf16[8,64,128]{2,1,0:T(8,128)(2,1)S(1)}, bf16[8,64,128]{2,1,0:T(8,128)(2,1)S(1)}, u32[]{:S(2)}, u32[]{:S(2)}) collective-permute-start(bf16[8,64,128]{2,1,0:T(8,128)(2,1)S(1)} %all_to_all.27.own), channel_id=1, source_target_pairs={{0,1},{1,0},{2,3},{3,2},{4,5},{5,4},{6,7},{7,6},{8,9},{9,8},{10,11... | collective-permute-start | bytes 393224 | tf_op jit(solution)/shard_map/ppermute | solution.py:34

commit v3 on v2

v3 whole, which is shorter than its diff:
```python
import functools
import math

import jax
import jax.numpy as jnp
from jax import lax
from jax.experimental import pallas as pl
from jax.experimental.pallas import tpu as pltpu
from jax.sharding import PartitionSpec as P


FEAT = 128
CLASSES = 64
LOG2E = math.log2(math.e)
CHUNK = 512
BF16 = jnp.bfloat16
F32 = jnp.float32


def z_groups(cols):
    return [[z * 4 + rest for z in range(cols // 4)] for rest in range(4)]


def facing(row):
    return (row + 4) % 8


def row_block_groups(rows, cols):
    return [
        [
            (facing(row) if y_hi else row) * cols + z * 4 + y_hi * 2 + core
            for y_hi in range(2)
            for z in range(cols // 4)
        ]
        for row in range(rows)
        for core in range(2)
    ]


def other_core(value, cols):
    return lax.ppermute(value, "col", [(col, col ^ 1) for col in range(cols)])


def facing_y(value, rows, cols):
    pairs = [
        (row * cols + col, facing(row) * cols + (col ^ 2))
        for row in range(rows)
        for col in range(cols)
    ]
    return lax.ppermute(value, ("row", "col"), pairs)


def extended(block, left):
    rows = block.shape[0]
    wide = block.astype(F32)
    square = jnp.sum(wide * wide, axis=1, keepdims=True) * (-1.0 / FEAT)
    first = square.astype(BF16).astype(F32)
    second = square - first
    lane = lax.broadcasted_iota(jnp.int32, (rows, FEAT), 1)
    at = 0 if left else 2
    ones = 2 - at
    extra = jnp.where((lane >= ones) & (lane < ones + 2), 1.0, 0.0)
    extra = jnp.where(lane == at, first, extra)
    extra = jnp.where(lane == at + 1, second, extra)
    scaled = block * jnp.asarray(2.0 / FEAT, BF16) if left else block
    return jnp.concatenate([scaled, extra.astype(BF16)], axis=1)


def side_by_side(values):
    return jnp.concatenate([values[g] for g in range(values.shape[0])], axis=1)


def build_part(packed, right_ext, tile):
    points = packed.shape[1] - CLASSES
    left = jnp.concatenate(
        [extended(packed[g, :points, :], True) for g in range(packed.shape[0])], axis=0
    )
    for start in range(0, tile.shape[1], CHUNK):
        exponent = lax.dot_general(
            left,
            right_ext[start : start + CHUNK, :],
            (((1,), (1,)), ((), ())),
            preferred_element_type=F32,
        )
        tile[:, start : start + CHUNK] = jnp.exp2(exponent * LOG2E).astype(BF16)
    return jnp.dot(
        side_by_side(packed[:, points:, :]), tile[...], preferred_element_type=F32
    )


def write_blocks(total, sums):
    count, _, points = sums.shape
    for k in range(count):
        sums[k] = total[:, k * points : (k + 1) * points]


def first_kernel(packed, right, tile, right_ext, total):
    count, points, _ = right.shape
    for k in range(count):
        right_ext[k * points : (k + 1) * points, :] = extended(right[k], False)
    total[...] = build_part(packed, right_ext, tile)


def next_kernel(packed, right_ext, before, tile, total):
    total[...] = before[...] + build_part(packed, right_ext, tile)


def last_kernel(packed, right_ext, before, tile, sums):
    write_blocks(before[...] + build_part(packed, right_ext, tile), sums)


def tile_part(body, out_shape, rows, width, *operands):
    return pl.pallas_call(
        body,
        out_shape=[jax.ShapeDtypeStruct((rows, width), BF16), *out_shape],
        compiler_params=pltpu.CompilerParams(vmem_limit_bytes=16 << 20),
        cost_estimate=pl.CostEstimate(
            flops=4 * rows * width * FEAT, bytes_accessed=0, transcendentals=rows * width
        ),
    )(*operands)


def apply_kernel(own, other, own_near, own_far, other_near, other_far, sums):
    near = (lax.axis_index("col") // 2) % 2
    total = jnp.dot(side_by_side(own[near]), own_near[...], preferred_element_type=F32)
    total += jnp.dot(side_by_side(own[1 - near]), own_far[...], preferred_element_type=F32)
    total += jnp.dot(side_by_side(other[near]), other_near[...], preferred_element_type=F32)
    total += jnp.dot(side_by_side(other[1 - near]), other_far[...], preferred_element_type=F32)
    write_blocks(total, sums)


def apply_tile(own, other, tile, count):
    points = tile[0].shape[1] // count
    return pl.pallas_call(
        apply_kernel,
        out_shape=jax.ShapeDtypeStruct((count, CLASSES, points), F32),
        compiler_params=pltpu.CompilerParams(vmem_limit_bytes=16 << 20),
        name="apply_tile",
    )(own, other, *tile)


def pack_kernel(points, current, labels, packed, near, kept, kept_labels, wide, sems):
    rows = points.shape[0]
    copies = [
        pltpu.make_async_copy(source, target, sems.at[k])
        for k, (source, target) in enumerate(
            ((points, wide), (current, kept), (labels, kept_labels))
        )
    ]
    for copy in copies:
        copy.start()
    copies[0].wait()
    narrow = wide[...].astype(BF16)
    for k in range(near.shape[0]):
        near[k] = narrow
    for k in range(packed.shape[0]):
        packed[k, :rows] = narrow
    copies[1].wait()
    values = kept[...].astype(BF16)
    for k in range(packed.shape[0]):
        packed[k, rows:] = values
    copies[2].wait()


def pack(points, current, labels, zs, rights):
    rows = points.shape[0]
    in_hbm = pl.BlockSpec(memory_space=pltpu.HBM)
    in_vmem = pl.BlockSpec(memory_space=pltpu.VMEM)
    return pl.pallas_call(
        pack_kernel,
        in_specs=[in_hbm] * 3,
        out_specs=[in_vmem] * 4,
        out_shape=[
            jax.ShapeDtypeStruct((zs, rows + CLASSES, FEAT), BF16),
            jax.ShapeDtypeStruct((rights, rows, FEAT), BF16),
            jax.ShapeDtypeStruct(current.shape, F32),
            jax.ShapeDtypeStruct(labels.shape, jnp.int32),
        ],
        scratch_shapes=[pltpu.VMEM(points.shape, F32), pltpu.SemaphoreType.DMA((3,))],
        compiler_params=pltpu.CompilerParams(vmem_limit_bytes=8 << 20),
        name="pack",
    )(*(pltpu.with_memory_space_constraint(v, pltpu.HBM) for v in (points, current, labels)))


def softmax_kernel(logit_scale, parts, labels, residual, probabilities):
    logits = logit_scale * jnp.sum(parts[...], axis=0)
    raised = jnp.exp(logits - jnp.max(logits, axis=0, keepdims=True))
    value = raised / jnp.sum(raised, axis=0, keepdims=True)
    classes = lax.broadcasted_iota(jnp.int32, value.shape, 0)
    onehot = jnp.where(classes == labels[...], 1.0, 0.0)
    change = (logit_scale * (value - onehot)).astype(BF16)
    probabilities[...] = value
    for k in range(residual.shape[0]):
        residual[k] = change


def softmax_and_residual(parts, labels, logit_scale, zs):
    _, classes, points = parts.shape
    return pl.pallas_call(
        functools.partial(softmax_kernel, logit_scale),
        out_shape=[
            jax.ShapeDtypeStruct((zs, classes, points), BF16),
            jax.ShapeDtypeStruct((classes, points), F32),
        ],
        compiler_params=pltpu.CompilerParams(vmem_limit_bytes=8 << 20),
        name="softmax_and_residual",
    )(parts, labels)


def finish_kernel(parts, current, probabilities, new_current, out_probabilities):
    new_current[...] = current[...] - jnp.sum(parts[...], axis=0)
    out_probabilities[...] = probabilities[...]


def finish(parts, current, probabilities):
    shape = jax.ShapeDtypeStruct(current.shape, F32)
    return pl.pallas_call(
        finish_kernel,
        out_shape=[shape, shape],
        compiler_params=pltpu.CompilerParams(vmem_limit_bytes=8 << 20),
        name="finish",
    )(parts, current, probabilities)


def on_device(rows, cols, points, labels, coefficients):
    count = points.shape[0]
    logit_scale = 16.0 / math.sqrt(count * rows * cols)
    zs = cols // 4

    def over_rows(parts):
        return lax.all_to_all(parts, "row", 0, 0, tiled=True)

    current = coefficients.T
    packed, near, current, labels = pack(points, current, labels[None, :], zs, rows)
    own_near = lax.all_to_all(
        packed, "col", 0, 0, tiled=True, axis_index_groups=z_groups(cols)
    )
    own_far = facing_y(own_near, rows, cols)
    other_near = other_core(own_near, cols)
    right = over_rows(near)
    high, width = zs * count, rows * count
    total = jax.ShapeDtypeStruct((CLASSES, width), F32)
    right_ext = jax.ShapeDtypeStruct((width, 2 * FEAT), BF16)
    own_near_tile, right_ext, total = tile_part(
        first_kernel, [right_ext, total], high, width, own_near, right
    )
    other_near_tile, total = tile_part(
        next_kernel, [total], high, width, other_near, right_ext, total
    )
    other_far = other_core(own_far, cols)
    own_far_tile, total = tile_part(next_kernel, [total], high, width, own_far, right_ext, total)
    sums = jax.ShapeDtypeStruct((rows, CLASSES, count), F32)
    other_far_tile, sums = tile_part(last_kernel, [sums], high, width, other_far, right_ext, total)
    tile = own_near_tile, own_far_tile, other_near_tile, other_far_tile
    residual, probabilities = softmax_and_residual(
        over_rows(sums), labels, logit_scale, 2 * zs
    )
    own = lax.all_to_all(
        residual,
        ("row", "col"),
        0,
        0,
        tiled=True,
        axis_index_groups=row_block_groups(rows, cols),
    ).reshape(2, zs, CLASSES, count)
    sums = apply_tile(own, other_core(own, cols), tile, rows)
    current, probabilities = finish(over_rows(sums), current, probabilities)
    return current.T, probabilities.T


def solution(mesh):
    rows, cols = mesh.shape["row"], mesh.shape["col"]
    return jax.shard_map(
        functools.partial(on_device, rows, cols),
        mesh=mesh,
        in_specs=(P(("row", "col"), None), P(("row", "col")), P(("row", "col"), None)),
        out_specs=(P(("row", "col"), None), P(("row", "col"), None)),
        check_vma=False,
    )
```

time: 90.9 us -> 92.2 us (1.014)
  the two profiles are of different devices: /device:TPU:16 before, /device:TPU:1 now
where the time goes in v3:
time: 92.2 us; the launch traced here: 91.9 us
  blocking collectives  66 us (72%)
  starting transfers between devices  11.4 us (12%)
  Pallas kernels  7.74 us (8%)
  waiting for transfers between devices  6.03 us (7%)
    all_to_all x3, blocking collectives, over_rows(): return lax.all_to_all(parts, 'row', 0, 0, tiled=True)  29.8 us
    all_to_all x1, blocking collectives, on_device(): lax.all_to_all(packed, 'col', 0, 0, tiled=True, axis_index_groups=z_group...  22.4 us
    all_to_all x1, blocking collectives, on_device(): lax.all_to_all(residual, ('row', 'col'), 0, 0, tiled=True, axis_index_gro...  13.8 us
    ppermute x3, starting transfers between devices, other_core(): return lax.ppermute(value, 'col', [(col, col ^ 1) for col in range(cols)])  8.66 us
    ppermute x1, waiting for transfers between devices, facing_y(): return lax.ppermute(value, ('row', 'col'), pairs)  4.87 us
    pallas_call x4, Pallas kernels, tile_part(): pl.pallas_call(body, out_shape=[jax.ShapeDtypeStruct((rows, width), BF16)...  4.54 us
    ppermute x1, starting transfers between devices, facing_y(): return lax.ppermute(value, ('row', 'col'), pairs)  2.73 us
  transfers between devices with their start and end apart: 4, of which 2 were waited for; matrix products, arithmetic and copies ran while one was open for 0% of the time, Pallas kernels for 4%

profile of v3, /device:TPU:1, one launch (start us, length us, event | category | flops | bytes accessed | tf_op | source)
XLA Modules:
  0.0 91.9 jit_solution(1288428810536658578)
XLA Ops:
  0.6 0.9 %pack.1 = (bf16[8,192,128]{2,1,0:T(8,128)(2,1)S(1)}, bf16[8,128,128]{2,1,0:T(8,128)(2,1)S(1)}, f32[64,128]{1,0:T(8,128)S(1)}, s32[1,128]{1,0:T(1,128)S(1)}) custom-call(f32[128,128]{1,0:T(8,128)} %points.1, f32[64,128]{1,0:T(8,128)} %bitcast.7, s32[1,128]{1,0:T(1,128)} %bitcast.8), custom_call_target="tpu_custom_call" | custom-call | tf_op jit(solution)/shard_map/pack/pallas_call | solution.py:169
  1.6 22.4 %all_to_all.25.packed = bf16[8,192,128]{2,1,0:T(8,128)(2,1)S(1)} all-to-all(bf16[8,192,128]{2,1,0:T(8,128)(2,1)S(1)} %get-tuple-element.19), channel_id=1, replica_groups={{0,4,8,12,16,20,24,28},{1,5,9,13,17,21,25,29},{2,6,10,14,18,22,26,30},{..., dimensions={0} | all-to-all | bytes 786432 | tf_op jit(solution)/shard_map/all_to_all | solution.py:235
  23.9 2.7 %collective-permute-start = (bf16[8,192,128]{2,1,0:T(8,128)(2,1)S(1)}, bf16[8,192,128]{2,1,0:T(8,128)(2,1)S(1)}, u32[]{:S(2)}, u32[]{:S(2)}) collective-permute-start(bf16[8,192,128]{2,1,0:T(8,128)(2,1)S(1)} %all_to_all.25.packed), channel_id=1, source_target_pairs={{0,130},{1,131},{2,128},{3,129},{4,134},{5,135},{6,132},{7,133},{8... | collective-permute-start | bytes 1179656 | tf_op jit(solution)/shard_map/ppermute | solution.py:50
  26.7 2.3 %collective-permute-start.2 = (bf16[8,192,128]{2,1,0:T(8,128)(2,1)S(1)}, bf16[8,192,128]{2,1,0:T(8,128)(2,1)S(1)}, u32[]{:S(2)}, u32[]{:S(2)}) collective-permute-start(bf16[8,192,128]{2,1,0:T(8,128)(2,1)S(1)} %all_to_all.25.packed), channel_id=1, source_target_pairs={{0,1},{1,0},{2,3},{3,2},{4,5},{5,4},{6,7},{7,6},{8,9},{9,8},{10,11... | collective-permute-start | bytes 1179656 | tf_op jit(solution)/shard_map/ppermute | solution.py:41
  29.0 4.9 %collective-permute-done.packed = bf16[8,192,128]{2,1,0:T(8,128)(2,1)S(1)} collective-permute-done((bf16[8,192,128]{2,1,0:T(8,128)(2,1)S(1)}, bf16[8,192,128]{2,1,0:T(8,128)(2,1)S(1)}, u32[]{:S(2)}, u32[]{:S(2)}) %collective-permute-start) | collective-permute-done | bytes 393248 | tf_op jit(solution)/shard_map/ppermute | solution.py:50
  33.9 2.9 %collective-permute-start.1 = (bf16[8,192,128]{2,1,0:T(8,128)(2,1)S(1)}, bf16[8,192,128]{2,1,0:T(8,128)(2,1)S(1)}, u32[]{:S(2)}, u32[]{:S(2)}) collective-permute-start(bf16[8,192,128]{2,1,0:T(8,128)(2,1)S(1)} %collective-permute-done.packed), channel_id=1, source_target_pairs={{0,1},{1,0},{2,3},{3,2},{4,5},{5,4},{6,7},{7,6},{8,9},{9,8},{10,11... | collective-permute-start | bytes 1179656 | tf_op jit(solution)/shard_map/ppermute | solution.py:41
  36.8 11.2 %all_to_all.26.right = bf16[8,128,128]{2,1,0:T(8,128)(2,1)S(1)} all-to-all(bf16[8,128,128]{2,1,0:T(8,128)(2,1)S(1)} %get-tuple-element.20), channel_id=1, replica_groups=mesh['row'=8,'col'=32] {'row'}, dimensions={0} | all-to-all | bytes 524288 | tf_op jit(solution)/shard_map/all_to_all | solution.py:231
  48.0 1.2 %shard_map.50 = (bf16[1024,1024]{1,0:T(8,128)(2,1)S(1)}, bf16[1024,256]{1,0:T(8,128)(2,1)S(1)}, f32[64,1024]{1,0:T(8,128)S(1)}) custom-call(bf16[8,192,128]{2,1,0:T(8,128)(2,1)S(1)} %all_to_all.25.packed, bf16[8,128,128]{2,1,0:T(8,128)(2,1)S(1)} %all_to_all.26.right), custom_call_target="tpu_custom_call" | custom-call | flops 536870912 | tf_op jit(solution)/shard_map/pallas_call | solution.py:113
  49.2 0.0 collective-permute-done.2.packed
  49.2 1.1 %shard_map.51 = (bf16[1024,1024]{1,0:T(8,128)(2,1)S(1)}, f32[64,1024]{1,0:T(8,128)S(1)}) custom-call(bf16[8,192,128]{2,1,0:T(8,128)(2,1)S(1)} %collective-permute-done.2.packed, bf16[1024,256]{1,0:T(8,128)(2,1)S(1)} %get-tuple-element.21.right_ext, f32[64,1024]{1,0:T(8,128)S(1)} %get-tuple-element.22.before), custom_call_target="tpu_custom_call" | custom-call | flops 536870912 | tf_op jit(solution)/shard_map/pallas_call | solution.py:113
  50.3 1.1 %shard_map.52 = (bf16[1024,1024]{1,0:T(8,128)(2,1)S(1)}, f32[64,1024]{1,0:T(8,128)S(1)}) custom-call(bf16[8,192,128]{2,1,0:T(8,128)(2,1)S(1)} %collective-permute-done.packed, bf16[1024,256]{1,0:T(8,128)(2,1)S(1)} %get-tuple-element.21.right_ext, f32[64,1024]{1,0:T(8,128)S(1)} %get-tuple-element.23.before), custom_call_target="tpu_custom_call" | custom-call | flops 536870912 | tf_op jit(solution)/shard_map/pallas_call | solution.py:113
  51.4 0.0 collective-permute-done.1.packed
  51.5 1.1 %shard_map.53 = (bf16[1024,1024]{1,0:T(8,128)(2,1)S(1)}, f32[8,64,128]{2,1,0:T(8,128)S(1)}) custom-call(bf16[8,192,128]{2,1,0:T(8,128)(2,1)S(1)} %collective-permute-done.1.packed, bf16[1024,256]{1,0:T(8,128)(2,1)S(1)} %get-tuple-element.21.right_ext, f32[64,1024]{1,0:T(8,128)S(1)} %get-tuple-element.24.before), custom_call_target="tpu_custom_call" | custom-call | flops 536870912 | tf_op jit(solution)/shard_map/pallas_call | solution.py:113
  52.6 8.7 %all_to_all.27.parts = f32[8,64,128]{2,1,0:T(8,128)S(1)} all-to-all(f32[8,64,128]{2,1,0:T(8,128)S(1)} %get-tuple-element.25), channel_id=1, replica_groups=mesh['row'=8,'col'=32] {'row'}, dimensions={0} | all-to-all | bytes 524288 | tf_op jit(solution)/shard_map/all_to_all | solution.py:231
  61.3 0.1 softmax_and_residual.1
  61.4 13.8 %all_to_all.28 = bf16[16,64,128]{2,1,0:T(8,128)(2,1)S(1)} all-to-all(bf16[16,64,128]{2,1,0:T(8,128)(2,1)S(1)} %get-tuple-element.27), channel_id=1, replica_groups={{0,4,8,12,16,20,24,28,130,134,138,142,146,150,154,158},{1,5,9,13,17,21,..., dimensions={0} | all-to-all | bytes 524288 | tf_op jit(solution)/shard_map/all_to_all | solution.py:258
  75.2 3.5 %collective-permute-start.3 = (bf16[2,8,64,128]{3,2,1,0:T(8,128)(2,1)S(1)}, bf16[2,8,64,128]{3,2,1,0:T(8,128)(2,1)S(1)}, u32[]{:S(2)}, u32[]{:S(2)}) collective-permute-start(bf16[2,8,64,128]{3,2,1,0:T(8,128)(2,1)S(1)} %bitcast.5), channel_id=1, source_target_pairs={{0,1},{1,0},{2,3},{3,2},{4,5},{5,4},{6,7},{7,6},{8,9},{9,8},{10,11... | collective-permute-start | bytes 786440 | tf_op jit(solution)/shard_map/ppermute | solution.py:41
  78.7 1.2 %collective-permute-done.3.other = bf16[2,8,64,128]{3,2,1,0:T(8,128)(2,1)S(1)} collective-permute-done((bf16[2,8,64,128]{3,2,1,0:T(8,128)(2,1)S(1)}, bf16[2,8,64,128]{3,2,1,0:T(8,128)(2,1)S(1)}, u32[]{:S(2)}, u32[]{:S(2)}) %collective-permute-start.3) | collective-permute-done | bytes 262176 | tf_op jit(solution)/shard_map/ppermute | solution.py:41
  79.8 1.6 %apply_tile.1 = f32[8,64,128]{2,1,0:T(8,128)S(1)} custom-call(bf16[2,8,64,128]{3,2,1,0:T(8,128)(2,1)S(1)} %bitcast.6, bf16[2,8,64,128]{3,2,1,0:T(8,128)(2,1)S(1)} %collective-permute-done.3.other, bf16[1024,1024]{1,0:T(8,128)(2,1)S(1)} %get-tuple-element.28.own_near, bf16[1024,1024]{1,0:T(8,128)(2,1)S(1)} %get-tuple-element.29.own_far, ...), custom_call_target="tpu_custom_call" | custom-call | tf_op jit(solution)/shard_map/apply_tile/pallas_call | solution.py:134
  81.4 9.8 %all_to_all.29.parts = f32[8,64,128]{2,1,0:T(8,128)S(1)} all-to-all(f32[8,64,128]{2,1,0:T(8,128)S(1)} %apply_tile.1), channel_id=1, replica_groups=mesh['row'=8,'col'=32] {'row'}, dimensions={0} | all-to-all | bytes 524288 | tf_op jit(solution)/shard_map/all_to_all | solution.py:231
  91.2 0.6 finish.1
Async XLA Ops:
  23.9 9.9 %collective-permute-start = (bf16[8,192,128]{2,1,0:T(8,128)(2,1)S(1)}, bf16[8,192,128]{2,1,0:T(8,128)(2,1)S(1)}, u32[]{:S(2)}, u32[]{:S(2)}) collective-permute-start(bf16[8,192,128]{2,1,0:T(8,128)(2,1)S(1)} %all_to_all.25.packed), channel_id=1, source_target_pairs={{0,130},{1,131},{2,128},{3,129},{4,134},{5,135},{6,132},{7,133},{8... | collective-permute-start | bytes 1179656 | tf_op jit(solution)/shard_map/ppermute | solution.py:50
  26.7 22.5 %collective-permute-start.2 = (bf16[8,192,128]{2,1,0:T(8,128)(2,1)S(1)}, bf16[8,192,128]{2,1,0:T(8,128)(2,1)S(1)}, u32[]{:S(2)}, u32[]{:S(2)}) collective-permute-start(bf16[8,192,128]{2,1,0:T(8,128)(2,1)S(1)} %all_to_all.25.packed), channel_id=1, source_target_pairs={{0,1},{1,0},{2,3},{3,2},{4,5},{5,4},{6,7},{7,6},{8,9},{9,8},{10,11... | collective-permute-start | bytes 1179656 | tf_op jit(solution)/shard_map/ppermute | solution.py:41
  33.9 17.6 %collective-permute-start.1 = (bf16[8,192,128]{2,1,0:T(8,128)(2,1)S(1)}, bf16[8,192,128]{2,1,0:T(8,128)(2,1)S(1)}, u32[]{:S(2)}, u32[]{:S(2)}) collective-permute-start(bf16[8,192,128]{2,1,0:T(8,128)(2,1)S(1)} %collective-permute-done.packed), channel_id=1, source_target_pairs={{0,1},{1,0},{2,3},{3,2},{4,5},{5,4},{6,7},{7,6},{8,9},{9,8},{10,11... | collective-permute-start | bytes 1179656 | tf_op jit(solution)/shard_map/ppermute | solution.py:41
  75.2 4.6 %collective-permute-start.3 = (bf16[2,8,64,128]{3,2,1,0:T(8,128)(2,1)S(1)}, bf16[2,8,64,128]{3,2,1,0:T(8,128)(2,1)S(1)}, u32[]{:S(2)}, u32[]{:S(2)}) collective-permute-start(bf16[2,8,64,128]{3,2,1,0:T(8,128)(2,1)S(1)} %bitcast.5), channel_id=1, source_target_pairs={{0,1},{1,0},{2,3},{3,2},{4,5},{5,4},{6,7},{7,6},{8,9},{9,8},{10,11... | collective-permute-start | bytes 786440 | tf_op jit(solution)/shard_map/ppermute | solution.py:41

commit v4 on v3

--- a/solution.py
+++ b/solution.py
@@ -120,23 +120,31 @@
     )(*operands)
 
 
-def apply_kernel(own, other, own_near, own_far, other_near, other_far, sums):
+def product(values, near_tile, far_tile):
     near = (lax.axis_index("col") // 2) % 2
-    total = jnp.dot(side_by_side(own[near]), own_near[...], preferred_element_type=F32)
-    total += jnp.dot(side_by_side(own[1 - near]), own_far[...], preferred_element_type=F32)
-    total += jnp.dot(side_by_side(other[near]), other_near[...], preferred_element_type=F32)
-    total += jnp.dot(side_by_side(other[1 - near]), other_far[...], preferred_element_type=F32)
-    write_blocks(total, sums)
-
-
-def apply_tile(own, other, tile, count):
-    points = tile[0].shape[1] // count
-    return pl.pallas_call(
-        apply_kernel,
-        out_shape=jax.ShapeDtypeStruct((count, CLASSES, points), F32),
+    return jnp.dot(
+        side_by_side(values[near]), near_tile[...], preferred_element_type=F32
+    ) + jnp.dot(side_by_side(values[1 - near]), far_tile[...], preferred_element_type=F32)
+
+
+def apply_own_kernel(values, near_tile, far_tile, total):
+    total[...] = product(values, near_tile, far_tile)
+
+
+def apply_other_kernel(values, near_tile, far_tile, before, sums):
+    write_blocks(before[...] + product(values, near_tile, far_tile), sums)
+
+
+def apply_part(body, out_shape, *operands):
+    rows, width = operands[1].shape
+    return pl.pallas_call(
+        body,
+        out_shape=out_shape,
         compiler_params=pltpu.CompilerParams(vmem_limit_bytes=16 << 20),
-        name="apply_tile",
-    )(own, other, *tile)
+        cost_estimate=pl.CostEstimate(
+            flops=4 * rows * width * CLASSES, bytes_accessed=0, transcendentals=0
+        ),
+    )(*operands)
 
 
 def pack_kernel(points, current, labels, packed, near, kept, kept_labels, wide, sems):
@@ -239,19 +247,22 @@
     other_near = other_core(own_near, cols)
     right = over_rows(near)
     high, width = zs * count, rows * count
-    total = jax.ShapeDtypeStruct((CLASSES, width), F32)
+    total_shape = jax.ShapeDtypeStruct((CLASSES, width), F32)
     right_ext = jax.ShapeDtypeStruct((width, 2 * FEAT), BF16)
     own_near_tile, right_ext, total = tile_part(
-        first_kernel, [right_ext, total], high, width, own_near, right
+        first_kernel, [right_ext, total_shape], high, width, own_near, right
     )
     other_near_tile, total = tile_part(
-        next_kernel, [total], high, width, other_near, right_ext, total
+        next_kernel, [total_shape], high, width, other_near, right_ext, total
     )
     other_far = other_core(own_far, cols)
-    own_far_tile, total = tile_part(next_kernel, [total], high, width, own_far, right_ext, total)
-    sums = jax.ShapeDtypeStruct((rows, CLASSES, count), F32)
-    other_far_tile, sums = tile_part(last_kernel, [sums], high, width, other_far, right_ext, total)
-    tile = own_near_tile, own_far_tile, other_near_tile, other_far_tile
+    own_far_tile, total = tile_part(
+        next_kernel, [total_shape], high, width, own_far, right_ext, total
+    )
+    sums_shape = jax.ShapeDtypeStruct((rows, CLASSES, count), F32)
+    other_far_tile, sums = tile_part(
+        last_kernel, [sums_shape], high, width, other_far, right_ext, total
+    )
     residual, probabilities = softmax_and_residual(
         over_rows(sums), labels, logit_scale, 2 * zs
     )
@@ -263,7 +274,9 @@
         tiled=True,
         axis_index_groups=row_block_groups(rows, cols),
     ).reshape(2, zs, CLASSES, count)
-    sums = apply_tile(own, other_core(own, cols), tile, rows)
+    other = other_core(own, cols)
+    total = apply_part(apply_own_kernel, total_shape, own, own_near_tile, own_far_tile)
+    sums = apply_part(apply_other_kernel, sums_shape, other, other_near_tile, other_far_tile, total)
     current, probabilities = finish(over_rows(sums), current, probabilities)
     return current.T, probabilities.T
 

time: 92.2 us -> 91.5 us (level)
  transfers between devices with their start and end apart: 4 -> 4, of which waited for: 2 -> 2; matrix products, arithmetic and copies ran while one was open for 0% -> 0% of each run, Pallas kernels for 4% -> 5%
where the time goes in v4:
time: 91.5 us; the launch traced here: 91.1 us
  blocking collectives  66 us (72%)
  starting transfers between devices  11.4 us (12%)
  Pallas kernels  7.85 us (9%)
  waiting for transfers between devices  5.2 us (6%)
    all_to_all x3, blocking collectives, over_rows(): return lax.all_to_all(parts, 'row', 0, 0, tiled=True)  29.8 us
    all_to_all x1, blocking collectives, on_device(): lax.all_to_all(packed, 'col', 0, 0, tiled=True, axis_index_groups=z_group...  22.4 us
    all_to_all x1, blocking collectives, on_device(): lax.all_to_all(residual, ('row', 'col'), 0, 0, tiled=True, axis_index_gro...  13.8 us
    ppermute x3, starting transfers between devices, other_core(): return lax.ppermute(value, 'col', [(col, col ^ 1) for col in range(cols)])  8.66 us
    ppermute x1, waiting for transfers between devices, facing_y(): return lax.ppermute(value, ('row', 'col'), pairs)  4.87 us
    pallas_call x4, Pallas kernels, tile_part(): pl.pallas_call(body, out_shape=[jax.ShapeDtypeStruct((rows, width), BF16)...  4.54 us
    ppermute x1, starting transfers between devices, facing_y(): return lax.ppermute(value, ('row', 'col'), pairs)  2.73 us
  transfers between devices with their start and end apart: 4, of which 2 were waited for; matrix products, arithmetic and copies ran while one was open for 0% of the time, Pallas kernels for 5%

profile of v4, /device:TPU:1, one launch (start us, length us, event | category | flops | bytes accessed | tf_op | source)
XLA Modules:
  0.0 91.1 jit_solution(2203575995262821014)
XLA Ops:
  0.6 0.9 %pack.1 = (bf16[8,192,128]{2,1,0:T(8,128)(2,1)S(1)}, bf16[8,128,128]{2,1,0:T(8,128)(2,1)S(1)}, f32[64,128]{1,0:T(8,128)S(1)}, s32[1,128]{1,0:T(1,128)S(1)}) custom-call(f32[128,128]{1,0:T(8,128)} %points.1, f32[64,128]{1,0:T(8,128)} %bitcast.7, s32[1,128]{1,0:T(1,128)} %bitcast.8), custom_call_target="tpu_custom_call" | custom-call | tf_op jit(solution)/shard_map/pack/pallas_call | solution.py:177
  1.6 22.4 %all_to_all.25.packed = bf16[8,192,128]{2,1,0:T(8,128)(2,1)S(1)} all-to-all(bf16[8,192,128]{2,1,0:T(8,128)(2,1)S(1)} %get-tuple-element.19), channel_id=1, replica_groups={{0,4,8,12,16,20,24,28},{1,5,9,13,17,21,25,29},{2,6,10,14,18,22,26,30},{..., dimensions={0} | all-to-all | bytes 786432 | tf_op jit(solution)/shard_map/all_to_all | solution.py:243
  23.9 2.7 %collective-permute-start = (bf16[8,192,128]{2,1,0:T(8,128)(2,1)S(1)}, bf16[8,192,128]{2,1,0:T(8,128)(2,1)S(1)}, u32[]{:S(2)}, u32[]{:S(2)}) collective-permute-start(bf16[8,192,128]{2,1,0:T(8,128)(2,1)S(1)} %all_to_all.25.packed), channel_id=1, source_target_pairs={{0,130},{1,131},{2,128},{3,129},{4,134},{5,135},{6,132},{7,133},{8... | collective-permute-start | bytes 1179656 | tf_op jit(solution)/shard_map/ppermute | solution.py:50
  26.7 2.3 %collective-permute-start.2 = (bf16[8,192,128]{2,1,0:T(8,128)(2,1)S(1)}, bf16[8,192,128]{2,1,0:T(8,128)(2,1)S(1)}, u32[]{:S(2)}, u32[]{:S(2)}) collective-permute-start(bf16[8,192,128]{2,1,0:T(8,128)(2,1)S(1)} %all_to_all.25.packed), channel_id=1, source_target_pairs={{0,1},{1,0},{2,3},{3,2},{4,5},{5,4},{6,7},{7,6},{8,9},{9,8},{10,11... | collective-permute-start | bytes 1179656 | tf_op jit(solution)/shard_map/ppermute | solution.py:41
  29.0 4.9 %collective-permute-done.packed = bf16[8,192,128]{2,1,0:T(8,128)(2,1)S(1)} collective-permute-done((bf16[8,192,128]{2,1,0:T(8,128)(2,1)S(1)}, bf16[8,192,128]{2,1,0:T(8,128)(2,1)S(1)}, u32[]{:S(2)}, u32[]{:S(2)}) %collective-permute-start) | collective-permute-done | bytes 393248 | tf_op jit(solution)/shard_map/ppermute | solution.py:50
  33.9 2.9 %collective-permute-start.1 = (bf16[8,192,128]{2,1,0:T(8,128)(2,1)S(1)}, bf16[8,192,128]{2,1,0:T(8,128)(2,1)S(1)}, u32[]{:S(2)}, u32[]{:S(2)}) collective-permute-start(bf16[8,192,128]{2,1,0:T(8,128)(2,1)S(1)} %collective-permute-done.packed), channel_id=1, source_target_pairs={{0,1},{1,0},{2,3},{3,2},{4,5},{5,4},{6,7},{7,6},{8,9},{9,8},{10,11... | collective-permute-start | bytes 1179656 | tf_op jit(solution)/shard_map/ppermute | solution.py:41
  36.8 11.2 %all_to_all.26.right = bf16[8,128,128]{2,1,0:T(8,128)(2,1)S(1)} all-to-all(bf16[8,128,128]{2,1,0:T(8,128)(2,1)S(1)} %get-tuple-element.20), channel_id=1, replica_groups=mesh['row'=8,'col'=32] {'row'}, dimensions={0} | all-to-all | bytes 524288 | tf_op jit(solution)/shard_map/all_to_all | solution.py:239
  48.0 1.2 %shard_map.50 = (bf16[1024,1024]{1,0:T(8,128)(2,1)S(1)}, bf16[1024,256]{1,0:T(8,128)(2,1)S(1)}, f32[64,1024]{1,0:T(8,128)S(1)}) custom-call(bf16[8,192,128]{2,1,0:T(8,128)(2,1)S(1)} %all_to_all.25.packed, bf16[8,128,128]{2,1,0:T(8,128)(2,1)S(1)} %all_to_all.26.right), custom_call_target="tpu_custom_call" | custom-call | flops 536870912 | tf_op jit(solution)/shard_map/pallas_call | solution.py:113
  49.2 0.0 collective-permute-done.2.packed
  49.2 1.1 %shard_map.51 = (bf16[1024,1024]{1,0:T(8,128)(2,1)S(1)}, f32[64,1024]{1,0:T(8,128)S(1)}) custom-call(bf16[8,192,128]{2,1,0:T(8,128)(2,1)S(1)} %collective-permute-done.2.packed, bf16[1024,256]{1,0:T(8,128)(2,1)S(1)} %get-tuple-element.21.right_ext, f32[64,1024]{1,0:T(8,128)S(1)} %get-tuple-element.22.before), custom_call_target="tpu_custom_call" | custom-call | flops 536870912 | tf_op jit(solution)/shard_map/pallas_call | solution.py:113
  50.3 1.1 %shard_map.52 = (bf16[1024,1024]{1,0:T(8,128)(2,1)S(1)}, f32[64,1024]{1,0:T(8,128)S(1)}) custom-call(bf16[8,192,128]{2,1,0:T(8,128)(2,1)S(1)} %collective-permute-done.packed, bf16[1024,256]{1,0:T(8,128)(2,1)S(1)} %get-tuple-element.21.right_ext, f32[64,1024]{1,0:T(8,128)S(1)} %get-tuple-element.23.before), custom_call_target="tpu_custom_call" | custom-call | flops 536870912 | tf_op jit(solution)/shard_map/pallas_call | solution.py:113
  51.5 0.0 collective-permute-done.1.packed
  51.5 1.1 %shard_map.53 = (bf16[1024,1024]{1,0:T(8,128)(2,1)S(1)}, f32[8,64,128]{2,1,0:T(8,128)S(1)}) custom-call(bf16[8,192,128]{2,1,0:T(8,128)(2,1)S(1)} %collective-permute-done.1.packed, bf16[1024,256]{1,0:T(8,128)(2,1)S(1)} %get-tuple-element.21.right_ext, f32[64,1024]{1,0:T(8,128)S(1)} %get-tuple-element.24.before), custom_call_target="tpu_custom_call" | custom-call | flops 536870912 | tf_op jit(solution)/shard_map/pallas_call | solution.py:113
  52.6 8.7 %all_to_all.27.parts = f32[8,64,128]{2,1,0:T(8,128)S(1)} all-to-all(f32[8,64,128]{2,1,0:T(8,128)S(1)} %get-tuple-element.25), channel_id=1, replica_groups=mesh['row'=8,'col'=32] {'row'}, dimensions={0} | all-to-all | bytes 524288 | tf_op jit(solution)/shard_map/all_to_all | solution.py:239
  61.3 0.1 softmax_and_residual.1
  61.4 13.8 %all_to_all.28 = bf16[16,64,128]{2,1,0:T(8,128)(2,1)S(1)} all-to-all(bf16[16,64,128]{2,1,0:T(8,128)(2,1)S(1)} %get-tuple-element.27), channel_id=1, replica_groups={{0,4,8,12,16,20,24,28,130,134,138,142,146,150,154,158},{1,5,9,13,17,21,..., dimensions={0} | all-to-all | bytes 524288 | tf_op jit(solution)/shard_map/all_to_all | solution.py:269
  75.2 3.5 %collective-permute-start.3 = (bf16[2,8,64,128]{3,2,1,0:T(8,128)(2,1)S(1)}, bf16[2,8,64,128]{3,2,1,0:T(8,128)(2,1)S(1)}, u32[]{:S(2)}, u32[]{:S(2)}) collective-permute-start(bf16[2,8,64,128]{3,2,1,0:T(8,128)(2,1)S(1)} %bitcast.5), channel_id=1, source_target_pairs={{0,1},{1,0},{2,3},{3,2},{4,5},{5,4},{6,7},{7,6},{8,9},{9,8},{10,11... | collective-permute-start | bytes 786440 | tf_op jit(solution)/shard_map/ppermute | solution.py:41
  78.7 0.8 shard_map.54.before
  79.5 0.3 collective-permute-done.3.values
  79.8 0.8 shard_map.55
  80.7 9.8 %all_to_all.29.parts = f32[8,64,128]{2,1,0:T(8,128)S(1)} all-to-all(f32[8,64,128]{2,1,0:T(8,128)S(1)} %shard_map.55), channel_id=1, replica_groups=mesh['row'=8,'col'=32] {'row'}, dimensions={0} | all-to-all | bytes 524288 | tf_op jit(solution)/shard_map/all_to_all | solution.py:239
  90.5 0.6 finish.1
Async XLA Ops:
  23.9 9.9 %collective-permute-start = (bf16[8,192,128]{2,1,0:T(8,128)(2,1)S(1)}, bf16[8,192,128]{2,1,0:T(8,128)(2,1)S(1)}, u32[]{:S(2)}, u32[]{:S(2)}) collective-permute-start(bf16[8,192,128]{2,1,0:T(8,128)(2,1)S(1)} %all_to_all.25.packed), channel_id=1, source_target_pairs={{0,130},{1,131},{2,128},{3,129},{4,134},{5,135},{6,132},{7,133},{8... | collective-permute-start | bytes 1179656 | tf_op jit(solution)/shard_map/ppermute | solution.py:50
  26.7 22.5 %collective-permute-start.2 = (bf16[8,192,128]{2,1,0:T(8,128)(2,1)S(1)}, bf16[8,192,128]{2,1,0:T(8,128)(2,1)S(1)}, u32[]{:S(2)}, u32[]{:S(2)}) collective-permute-start(bf16[8,192,128]{2,1,0:T(8,128)(2,1)S(1)} %all_to_all.25.packed), channel_id=1, source_target_pairs={{0,1},{1,0},{2,3},{3,2},{4,5},{5,4},{6,7},{7,6},{8,9},{9,8},{10,11... | collective-permute-start | bytes 1179656 | tf_op jit(solution)/shard_map/ppermute | solution.py:41
  33.9 17.6 %collective-permute-start.1 = (bf16[8,192,128]{2,1,0:T(8,128)(2,1)S(1)}, bf16[8,192,128]{2,1,0:T(8,128)(2,1)S(1)}, u32[]{:S(2)}, u32[]{:S(2)}) collective-permute-start(bf16[8,192,128]{2,1,0:T(8,128)(2,1)S(1)} %collective-permute-done.packed), channel_id=1, source_target_pairs={{0,1},{1,0},{2,3},{3,2},{4,5},{5,4},{6,7},{7,6},{8,9},{9,8},{10,11... | collective-permute-start | bytes 1179656 | tf_op jit(solution)/shard_map/ppermute | solution.py:41
  75.2 4.6 %collective-permute-start.3 = (bf16[2,8,64,128]{3,2,1,0:T(8,128)(2,1)S(1)}, bf16[2,8,64,128]{3,2,1,0:T(8,128)(2,1)S(1)}, u32[]{:S(2)}, u32[]{:S(2)}) collective-permute-start(bf16[2,8,64,128]{3,2,1,0:T(8,128)(2,1)S(1)} %bitcast.5), channel_id=1, source_target_pairs={{0,1},{1,0},{2,3},{3,2},{4,5},{5,4},{6,7},{7,6},{8,9},{9,8},{10,11... | collective-permute-start | bytes 786440 | tf_op jit(solution)/shard_map/ppermute | solution.py:41

commit v5 on v4

--- a/solution.py
+++ b/solution.py
@@ -70,22 +70,36 @@
     return jnp.concatenate([values[g] for g in range(values.shape[0])], axis=1)
 
 
-def build_part(packed, right_ext, tile):
-    points = packed.shape[1] - CLASSES
-    left = jnp.concatenate(
-        [extended(packed[g, :points, :], True) for g in range(packed.shape[0])], axis=0
-    )
-    for start in range(0, tile.shape[1], CHUNK):
-        exponent = lax.dot_general(
-            left,
-            right_ext[start : start + CHUNK, :],
-            (((1,), (1,)), ((), ())),
-            preferred_element_type=F32,
+def build_parts(parts, right_ext, tiles, left_ext):
+    points = parts[0].shape[1] - CLASSES
+    blocks, width = parts[0].shape[0], tiles[0].shape[1]
+
+    def extend(part, block):
+        left_ext[part, block * points : (block + 1) * points, :] = extended(
+            parts[part][block, :points, :], True
         )
-        tile[:, start : start + CHUNK] = jnp.exp2(exponent * LOG2E).astype(BF16)
-    return jnp.dot(
-        side_by_side(packed[:, points:, :]), tile[...], preferred_element_type=F32
-    )
+
+    for block in range(blocks):
+        extend(0, block)
+    total = None
+    chunks = width // CHUNK
+    for part, tile in enumerate(tiles):
+        for chunk in range(chunks):
+            at = slice(chunk * CHUNK, (chunk + 1) * CHUNK)
+            exponent = lax.dot_general(
+                left_ext[part],
+                right_ext[at, :],
+                (((1,), (1,)), ((), ())),
+                preferred_element_type=F32,
+            )
+            tile[:, at] = jnp.exp2(exponent * LOG2E).astype(BF16)
+            if part + 1 < len(tiles):
+                for block in range(chunk * blocks // chunks, (chunk + 1) * blocks // chunks):
+                    extend(part + 1, block)
+        values = side_by_side(parts[part][:, points:, :])
+        added = jnp.dot(values, tile[...], preferred_element_type=F32)
+        total = added if total is None else total + added
+    return total
 
 
 def write_blocks(total, sums):
@@ -94,28 +108,27 @@
         sums[k] = total[:, k * points : (k + 1) * points]
 
 
-def first_kernel(packed, right, tile, right_ext, total):
+def own_kernel(near, far, right, near_tile, far_tile, right_ext, total, left_ext):
     count, points, _ = right.shape
     for k in range(count):
         right_ext[k * points : (k + 1) * points, :] = extended(right[k], False)
-    total[...] = build_part(packed, right_ext, tile)
-
-
-def next_kernel(packed, right_ext, before, tile, total):
-    total[...] = before[...] + build_part(packed, right_ext, tile)
-
-
-def last_kernel(packed, right_ext, before, tile, sums):
-    write_blocks(before[...] + build_part(packed, right_ext, tile), sums)
-
-
-def tile_part(body, out_shape, rows, width, *operands):
+    total[...] = build_parts((near, far), right_ext, (near_tile, far_tile), left_ext)
+
+
+def other_kernel(near, far, right_ext, before, near_tile, far_tile, sums, left_ext):
+    added = build_parts((near, far), right_ext, (near_tile, far_tile), left_ext)
+    write_blocks(before[...] + added, sums)
+
+
+def tile_parts(body, out_shape, rows, width, *operands):
+    part = jax.ShapeDtypeStruct((rows, width), BF16)
     return pl.pallas_call(
         body,
-        out_shape=[jax.ShapeDtypeStruct((rows, width), BF16), *out_shape],
+        out_shape=[part, part, *out_shape],
+        scratch_shapes=[pltpu.VMEM((2, rows, 2 * FEAT), BF16)],
         compiler_params=pltpu.CompilerParams(vmem_limit_bytes=16 << 20),
         cost_estimate=pl.CostEstimate(
-            flops=4 * rows * width * FEAT, bytes_accessed=0, transcendentals=rows * width
+            flops=8 * rows * width * FEAT, bytes_accessed=0, transcendentals=2 * rows * width
         ),
     )(*operands)
 
@@ -249,19 +262,13 @@
     high, width = zs * count, rows * count
     total_shape = jax.ShapeDtypeStruct((CLASSES, width), F32)
     right_ext = jax.ShapeDtypeStruct((width, 2 * FEAT), BF16)
-    own_near_tile, right_ext, total = tile_part(
-        first_kernel, [right_ext, total_shape], high, width, own_near, right
-    )
-    other_near_tile, total = tile_part(
-        next_kernel, [total_shape], high, width, other_near, right_ext, total
-    )
     other_far = other_core(own_far, cols)
-    own_far_tile, total = tile_part(
-        next_kernel, [total_shape], high, width, own_far, right_ext, total
+    own_near_tile, own_far_tile, right_ext, total = tile_parts(
+        own_kernel, [right_ext, total_shape], high, width, own_near, own_far, right
     )
     sums_shape = jax.ShapeDtypeStruct((rows, CLASSES, count), F32)
-    other_far_tile, sums = tile_part(
-        last_kernel, [sums_shape], high, width, other_far, right_ext, total
+    other_near_tile, other_far_tile, sums = tile_parts(
+        other_kernel, [sums_shape], high, width, other_near, other_far, right_ext, total
     )
     residual, probabilities = softmax_and_residual(
         over_rows(sums), labels, logit_scale, 2 * zs
@@ -276,7 +283,9 @@
     ).reshape(2, zs, CLASSES, count)
     other = other_core(own, cols)
     total = apply_part(apply_own_kernel, total_shape, own, own_near_tile, own_far_tile)
-    sums = apply_part(apply_other_kernel, sums_shape, other, other_near_tile, other_far_tile, total)
+    sums = apply_part(
+        apply_other_kernel, sums_shape, other, other_near_tile, other_far_tile, total
+    )
     current, probabilities = finish(over_rows(sums), current, probabilities)
     return current.T, probabilities.T
 

time: 91.5 us -> 91.3 us (level)
    pallas_call x4 -> x2, Pallas kernels: 4.54 us -> 4.42 us  [tile_parts(): pl.pallas_call(body, out_shape=[part, part, *out_shape], scratch_shapes=[...]
  transfers between devices with their start and end apart: 4 -> 4, of which waited for: 2 -> 2; matrix products, arithmetic and copies ran while one was open for 0% -> 0% of each run, Pallas kernels for 5% -> 3%
where the time goes in v5:
time: 91.3 us; the launch traced here: 91 us
  blocking collectives  66 us (72%)
  starting transfers between devices  11.4 us (12%)
  Pallas kernels  7.73 us (8%)
  waiting for transfers between devices  5.2 us (6%)
    all_to_all x3, blocking collectives, over_rows(): return lax.all_to_all(parts, 'row', 0, 0, tiled=True)  29.8 us
    all_to_all x1, blocking collectives, on_device(): lax.all_to_all(packed, 'col', 0, 0, tiled=True, axis_index_groups=z_group...  22.4 us
    all_to_all x1, blocking collectives, on_device(): lax.all_to_all(residual, ('row', 'col'), 0, 0, tiled=True, axis_index_gro...  13.8 us
    ppermute x3, starting transfers between devices, other_core(): return lax.ppermute(value, 'col', [(col, col ^ 1) for col in range(cols)])  8.66 us
    ppermute x1, waiting for transfers between devices, facing_y(): return lax.ppermute(value, ('row', 'col'), pairs)  4.87 us
    pallas_call x2, Pallas kernels, tile_parts(): pl.pallas_call(body, out_shape=[part, part, *out_shape], scratch_shapes=[...  4.42 us
    ppermute x1, starting transfers between devices, facing_y(): return lax.ppermute(value, ('row', 'col'), pairs)  2.73 us
  transfers between devices with their start and end apart: 4, of which 2 were waited for; matrix products, arithmetic and copies ran while one was open for 0% of the time, Pallas kernels for 3%

profile of v5, /device:TPU:1, one launch (start us, length us, event | category | flops | bytes accessed | tf_op | source)
XLA Modules:
  0.0 91.0 jit_solution(15729457412309437282)
XLA Ops:
  0.6 0.9 %pack.1 = (bf16[8,192,128]{2,1,0:T(8,128)(2,1)S(1)}, bf16[8,128,128]{2,1,0:T(8,128)(2,1)S(1)}, f32[64,128]{1,0:T(8,128)S(1)}, s32[1,128]{1,0:T(1,128)S(1)}) custom-call(f32[128,128]{1,0:T(8,128)} %points.1, f32[64,128]{1,0:T(8,128)} %bitcast.7, s32[1,128]{1,0:T(1,128)} %bitcast.8), custom_call_target="tpu_custom_call" | custom-call | tf_op jit(solution)/shard_map/pack/pallas_call | solution.py:190
  1.6 22.4 %all_to_all.25.near = bf16[8,192,128]{2,1,0:T(8,128)(2,1)S(1)} all-to-all(bf16[8,192,128]{2,1,0:T(8,128)(2,1)S(1)} %get-tuple-element.17), channel_id=1, replica_groups={{0,4,8,12,16,20,24,28},{1,5,9,13,17,21,25,29},{2,6,10,14,18,22,26,30},{..., dimensions={0} | all-to-all | bytes 786432 | tf_op jit(solution)/shard_map/all_to_all | solution.py:256
  23.9 2.7 %collective-permute-start.1 = (bf16[8,192,128]{2,1,0:T(8,128)(2,1)S(1)}, bf16[8,192,128]{2,1,0:T(8,128)(2,1)S(1)}, u32[]{:S(2)}, u32[]{:S(2)}) collective-permute-start(bf16[8,192,128]{2,1,0:T(8,128)(2,1)S(1)} %all_to_all.25.near), channel_id=1, source_target_pairs={{0,130},{1,131},{2,128},{3,129},{4,134},{5,135},{6,132},{7,133},{8... | collective-permute-start | bytes 1179656 | tf_op jit(solution)/shard_map/ppermute | solution.py:50
  26.7 2.3 %collective-permute-start = (bf16[8,192,128]{2,1,0:T(8,128)(2,1)S(1)}, bf16[8,192,128]{2,1,0:T(8,128)(2,1)S(1)}, u32[]{:S(2)}, u32[]{:S(2)}) collective-permute-start(bf16[8,192,128]{2,1,0:T(8,128)(2,1)S(1)} %all_to_all.25.near), channel_id=1, source_target_pairs={{0,1},{1,0},{2,3},{3,2},{4,5},{5,4},{6,7},{7,6},{8,9},{9,8},{10,11... | collective-permute-start | bytes 1179656 | tf_op jit(solution)/shard_map/ppermute | solution.py:41
  29.0 4.9 %collective-permute-done.1.far = bf16[8,192,128]{2,1,0:T(8,128)(2,1)S(1)} collective-permute-done((bf16[8,192,128]{2,1,0:T(8,128)(2,1)S(1)}, bf16[8,192,128]{2,1,0:T(8,128)(2,1)S(1)}, u32[]{:S(2)}, u32[]{:S(2)}) %collective-permute-start.1) | collective-permute-done | bytes 393248 | tf_op jit(solution)/shard_map/ppermute | solution.py:50
  33.9 2.9 %collective-permute-start.2 = (bf16[8,192,128]{2,1,0:T(8,128)(2,1)S(1)}, bf16[8,192,128]{2,1,0:T(8,128)(2,1)S(1)}, u32[]{:S(2)}, u32[]{:S(2)}) collective-permute-start(bf16[8,192,128]{2,1,0:T(8,128)(2,1)S(1)} %collective-permute-done.1.far), channel_id=1, source_target_pairs={{0,1},{1,0},{2,3},{3,2},{4,5},{5,4},{6,7},{7,6},{8,9},{9,8},{10,11... | collective-permute-start | bytes 1179656 | tf_op jit(solution)/shard_map/ppermute | solution.py:41
  36.8 11.2 %all_to_all.26.right = bf16[8,128,128]{2,1,0:T(8,128)(2,1)S(1)} all-to-all(bf16[8,128,128]{2,1,0:T(8,128)(2,1)S(1)} %get-tuple-element.18), channel_id=1, replica_groups=mesh['row'=8,'col'=32] {'row'}, dimensions={0} | all-to-all | bytes 524288 | tf_op jit(solution)/shard_map/all_to_all | solution.py:252
  48.0 2.3 %shard_map.50 = (bf16[1024,1024]{1,0:T(8,128)(2,1)S(1)}, bf16[1024,1024]{1,0:T(8,128)(2,1)S(1)}, bf16[1024,256]{1,0:T(8,128)(2,1)S(1)}, f32[64,1024]{1,0:T(8,128)S(1)}) custom-call(bf16[8,192,128]{2,1,0:T(8,128)(2,1)S(1)} %all_to_all.25.near, bf16[8,192,128]{2,1,0:T(8,128)(2,1)S(1)} %collective-permute-done.1.far, bf16[8,128,128]{2,1,0:T(8,128)(2,1)S(1)} %all_to_all.26.right), custom_call_target="tpu_custom_call" | custom-call | flops 1073741824 | tf_op jit(solution)/shard_map/pallas_call | solution.py:125
  50.3 0.0 collective-permute-done.near
  50.3 0.0 collective-permute-done.2.far
  50.3 2.1 %shard_map.51 = (bf16[1024,1024]{1,0:T(8,128)(2,1)S(1)}, bf16[1024,1024]{1,0:T(8,128)(2,1)S(1)}, f32[8,64,128]{2,1,0:T(8,128)S(1)}) custom-call(bf16[8,192,128]{2,1,0:T(8,128)(2,1)S(1)} %collective-permute-done.near, bf16[8,192,128]{2,1,0:T(8,128)(2,1)S(1)} %collective-permute-done.2.far, bf16[1024,256]{1,0:T(8,128)(2,1)S(1)} %get-tuple-element.19.right_ext, ...), custom_call_target="tpu_custom_call" | custom-call | flops 1073741824 | tf_op jit(solution)/shard_map/pallas_call | solution.py:125
  52.4 8.7 %all_to_all.27.parts = f32[8,64,128]{2,1,0:T(8,128)S(1)} all-to-all(f32[8,64,128]{2,1,0:T(8,128)S(1)} %get-tuple-element.21), channel_id=1, replica_groups=mesh['row'=8,'col'=32] {'row'}, dimensions={0} | all-to-all | bytes 524288 | tf_op jit(solution)/shard_map/all_to_all | solution.py:252
  61.1 0.1 softmax_and_residual.1
  61.2 13.8 %all_to_all.28 = bf16[16,64,128]{2,1,0:T(8,128)(2,1)S(1)} all-to-all(bf16[16,64,128]{2,1,0:T(8,128)(2,1)S(1)} %get-tuple-element.23), channel_id=1, replica_groups={{0,4,8,12,16,20,24,28,130,134,138,142,146,150,154,158},{1,5,9,13,17,21,..., dimensions={0} | all-to-all | bytes 524288 | tf_op jit(solution)/shard_map/all_to_all | solution.py:276
  75.0 3.5 %collective-permute-start.3 = (bf16[2,8,64,128]{3,2,1,0:T(8,128)(2,1)S(1)}, bf16[2,8,64,128]{3,2,1,0:T(8,128)(2,1)S(1)}, u32[]{:S(2)}, u32[]{:S(2)}) collective-permute-start(bf16[2,8,64,128]{3,2,1,0:T(8,128)(2,1)S(1)} %bitcast.5), channel_id=1, source_target_pairs={{0,1},{1,0},{2,3},{3,2},{4,5},{5,4},{6,7},{7,6},{8,9},{9,8},{10,11... | collective-permute-start | bytes 786440 | tf_op jit(solution)/shard_map/ppermute | solution.py:41
  78.5 0.8 shard_map.52.before
  79.3 0.3 collective-permute-done.3.values
  79.7 0.8 shard_map.53
  80.5 9.8 %all_to_all.29.parts = f32[8,64,128]{2,1,0:T(8,128)S(1)} all-to-all(f32[8,64,128]{2,1,0:T(8,128)S(1)} %shard_map.53), channel_id=1, replica_groups=mesh['row'=8,'col'=32] {'row'}, dimensions={0} | all-to-all | bytes 524288 | tf_op jit(solution)/shard_map/all_to_all | solution.py:252
  90.3 0.6 finish.1
Async XLA Ops:
  23.9 9.9 %collective-permute-start.1 = (bf16[8,192,128]{2,1,0:T(8,128)(2,1)S(1)}, bf16[8,192,128]{2,1,0:T(8,128)(2,1)S(1)}, u32[]{:S(2)}, u32[]{:S(2)}) collective-permute-start(bf16[8,192,128]{2,1,0:T(8,128)(2,1)S(1)} %all_to_all.25.near), channel_id=1, source_target_pairs={{0,130},{1,131},{2,128},{3,129},{4,134},{5,135},{6,132},{7,133},{8... | collective-permute-start | bytes 1179656 | tf_op jit(solution)/shard_map/ppermute | solution.py:50
  26.7 23.6 %collective-permute-start = (bf16[8,192,128]{2,1,0:T(8,128)(2,1)S(1)}, bf16[8,192,128]{2,1,0:T(8,128)(2,1)S(1)}, u32[]{:S(2)}, u32[]{:S(2)}) collective-permute-start(bf16[8,192,128]{2,1,0:T(8,128)(2,1)S(1)} %all_to_all.25.near), channel_id=1, source_target_pairs={{0,1},{1,0},{2,3},{3,2},{4,5},{5,4},{6,7},{7,6},{8,9},{9,8},{10,11... | collective-permute-start | bytes 1179656 | tf_op jit(solution)/shard_map/ppermute | solution.py:41
  33.9 16.4 %collective-permute-start.2 = (bf16[8,192,128]{2,1,0:T(8,128)(2,1)S(1)}, bf16[8,192,128]{2,1,0:T(8,128)(2,1)S(1)}, u32[]{:S(2)}, u32[]{:S(2)}) collective-permute-start(bf16[8,192,128]{2,1,0:T(8,128)(2,1)S(1)} %collective-permute-done.1.far), channel_id=1, source_target_pairs={{0,1},{1,0},{2,3},{3,2},{4,5},{5,4},{6,7},{7,6},{8,9},{9,8},{10,11... | collective-permute-start | bytes 1179656 | tf_op jit(solution)/shard_map/ppermute | solution.py:41
  75.0 4.6 %collective-permute-start.3 = (bf16[2,8,64,128]{3,2,1,0:T(8,128)(2,1)S(1)}, bf16[2,8,64,128]{3,2,1,0:T(8,128)(2,1)S(1)}, u32[]{:S(2)}, u32[]{:S(2)}) collective-permute-start(bf16[2,8,64,128]{3,2,1,0:T(8,128)(2,1)S(1)} %bitcast.5), channel_id=1, source_target_pairs={{0,1},{1,0},{2,3},{3,2},{4,5},{5,4},{6,7},{7,6},{8,9},{9,8},{10,11... | collective-permute-start | bytes 786440 | tf_op jit(solution)/shard_map/ppermute | solution.py:41
